TPU v7x, 256 devices: a whole 4x4x8 slice. The times are simulated.
256 devices in a mesh: seq: 32 (over z, y), mp: 8 (over x, core).
Axes of the slice: x: 4, y: 4, z: 8, core: 2. Of those that a mesh axis runs over, the one named last changes fastest.
Arguments:
- scored_token_targets: int32 [8192], P('seq'), may hold values from 0 to 15999
- valid: int32 [8192], P('seq'), may hold values 0 or 1
- lengths: int32 [48], replicated, may hold values from 1 to 1024, 8192 in all
- owners: int32 [48], replicated, may hold values from 0 to 31
- holders: int32 [48], replicated, may hold values from -1 to 31, as said below
- mixer_input_x: bfloat16 [2, 8192, 3584], P(None, 'seq', 'mp'), may hold values from -6 to 6
- mixer_gate_input: bfloat16 [2, 8192, 3584], P(None, 'seq', 'mp'), may hold values from -6 to 6
- input_projection_b: bfloat16 [2, 8192, 64], P(None, 'seq'), may hold values from -2.390625 to 2.390625
- output_projection_c: bfloat16 [2, 8192, 64], P(None, 'seq'), may hold values from -2.390625 to 2.390625
- token_step_sizes: float32 [2, 8192, 56], P(None, 'seq', 'mp'), may hold values from 0.01 to 0.3
- head_decay_rate: float32 [2, 56], P(None, 'mp'), may hold values from 0.0002 to 1
- head_skip_scale: float32 [2, 56], P(None, 'mp'), may hold values from 0.5 to 1.5
- prompt_held_states: bfloat16 [2, 32, 56, 64, 64], P(None, 'seq', 'mp'), may hold values from -6 to 6
- shared_output_weight: bfloat16 [3584, 3584], P('mp'), may hold values from -0.09375 to 0.09375
- adapter_down_weight: bfloat16 [3584, 128], P('mp'), may hold values from -0.09375 to 0.09375
- adapter_up_weight: bfloat16 [128, 3584], replicated, may hold values from -0.5 to 0.5
- residual: bfloat16 [8192, 2, 3584], P('seq'), may hold values from -16 to 16
- final_norm_scale: float32 [3584], replicated, may hold values from 0.5 to 1.5
- vocab_head_weight: bfloat16 [3584, 16000], P('seq', 'mp'), may hold values from -8 to 8
Outputs:
- owner_sums: float32 [32, 48], P('seq')
- token_delta: float32 [8192], P('seq')
Inputs may be any that keep to these rules, and one draw needn't show every extreme that they name: `holders`: exactly 24 rollouts continue a prompt state; the others start from zeros.
All inputs are finite; a program needn't handle non-finite values. No bound on the sum of `valid` on one device may be relied on, other than what follows from the above.
Results may differ from a plain program's by a relative error of at most 0.035.
Values may be sent and summed in bfloat16 or wider, within the bound.
A program may use at most 128 MiB of HBM per device.

v0:
```python
import jax
import jax.numpy as jnp
from jax import lax
from jax.sharding import PartitionSpec as P

highest = lax.Precision.HIGHEST


def shifted(x, axis, by):
    count = lax.axis_size(axis)
    pairs = [(i, i + by) for i in range(count) if 0 <= i + by < count]
    return lax.ppermute(x, axis, pairs)


def root_norm(hidden, final_norm_scale):
    mean_sq = jnp.mean(hidden * hidden, axis=-1, keepdims=True)
    return (hidden * lax.rsqrt(mean_sq + 1e-05) * final_norm_scale).astype(jnp.bfloat16)


def shards(
    scored_token_targets,
    valid,
    lengths,
    owners,
    holders,
    mixer_input_x,
    mixer_gate_input,
    input_projection_b,
    output_projection_c,
    token_step_sizes,
    head_decay_rate,
    head_skip_scale,
    prompt_held_states,
    shared_output_weight,
    adapter_down_weight,
    adapter_up_weight,
    residual,
    final_norm_scale,
    vocab_head_weight,
):
    seq_count = lax.axis_size("seq")
    mp_count = lax.axis_size("mp")
    tok_rows = scored_token_targets.shape[0]
    models = mixer_input_x.shape[0]
    inner_local = mixer_input_x.shape[2]
    head_count = token_step_sizes.shape[2]
    head_dim = inner_local // head_count
    state_dim = input_projection_b.shape[2]
    roll_count = lengths.shape[0]
    first_row = lax.axis_index("seq") * tok_rows
    offsets = jnp.arange(tok_rows, dtype=jnp.int32)
    position = first_row + offsets
    starts = jnp.cumsum(lengths) - lengths
    rollout = jnp.sum((starts[None, :] <= position[:, None]).astype(jnp.int32), axis=1) - 1
    member_table = rollout[:, None] == jnp.arange(roll_count, dtype=jnp.int32)[None, :]
    start_local = jnp.sum(jnp.where(member_table, starts[None, :], 0), axis=1) - first_row
    holder_tok = jnp.sum(jnp.where(member_table, holders[None, :], 0), axis=1)
    borrowed = (start_local >= 0) & (holder_tok >= 0)
    prompt_pick = (
        (holder_tok[:, None] == jnp.arange(seq_count, dtype=jnp.int32)[None, :]) & borrowed[:, None]
    ).astype(jnp.float32)
    neg_rates = -head_decay_rate
    log_decay = jnp.cumsum(token_step_sizes * neg_rates[:, None, :], axis=1)
    before = jnp.take(log_decay, jnp.maximum(start_local - 1, 0), axis=1)
    before = jnp.where((start_local >= 1)[None, :, None], before, 0.0)
    x_values = mixer_input_x.astype(jnp.float32).reshape(models, tok_rows, head_count, head_dim)
    b_values = input_projection_b.astype(jnp.float32)
    c_values = output_projection_c.astype(jnp.float32)
    gram_matrix = jnp.einsum(
        "mtn,msn->mts", output_projection_c, input_projection_b, preferred_element_type=jnp.float32
    )
    causal = (rollout[:, None] == rollout[None, :]) & (offsets[None, :] <= offsets[:, None])
    log_gap = log_decay[:, :, None, :] - log_decay[:, None, :, :]
    mixing = jnp.where(
        causal[None, :, :, None], jnp.exp(jnp.where(causal[None, :, :, None], log_gap, 0.0)), 0.0
    )
    mixing = mixing * gram_matrix[..., None] * token_step_sizes[:, None, :, :]
    intra_out = jnp.einsum("mtsh,mshp->mthp", mixing, x_values, precision=highest)
    last_pick = prompt_pick[tok_rows - 1]
    zeros_state = jnp.zeros((models, head_count, head_dim, state_dim), jnp.float32)
    piece = lax.all_gather(prompt_held_states, "seq", axis=1, tiled=True)
    last_weight = last_pick.astype(jnp.bfloat16)
    picked = (prompt_pick[None, :, :, None] * c_values[:, :, None, :]).astype(jnp.bfloat16)
    projected = jnp.einsum("mtjn,mjhpn->mthp", picked, piece, preferred_element_type=jnp.float32)
    end_states = jnp.einsum("j,mjhpn->mhpn", last_weight, piece, preferred_element_type=jnp.float32)
    entry_decay = jnp.exp(log_decay - before)
    final_log = log_decay[:, tok_rows - 1, :]
    tail_mask = (rollout == rollout[tok_rows - 1]).astype(jnp.float32)
    end_weight = (
        jnp.exp(final_log[:, None, :] - log_decay) * token_step_sizes * tail_mask[None, :, None]
    )
    local_end = jnp.einsum("msh,mshp,msn->mhpn", end_weight, x_values, b_values, precision=highest)
    local_end = (
        local_end + jnp.exp(final_log - before[:, tok_rows - 1, :])[:, :, None, None] * end_states
    )
    carry_through = jnp.where(start_local[tok_rows - 1] < 0, jnp.exp(final_log), 0.0)

    def relay_step(step_index, incoming):
        outgoing = carry_through[:, :, None, None] * incoming + local_end
        return shifted(outgoing, "seq", 1)

    arriving = lax.fori_loop(0, seq_count - 1, relay_step, zeros_state)
    inherited = (start_local < 0).astype(jnp.float32)
    carried = jnp.einsum("mhpn,mtn->mthp", arriving, c_values, precision=highest)
    carried = carried * (jnp.exp(log_decay) * inherited[None, :, None])[..., None]
    output = (
        intra_out
        + carried
        + entry_decay[..., None] * projected
        + head_skip_scale[:, None, :, None] * x_values
    )
    output = output.reshape(models, tok_rows, inner_local)
    gated_output = (output * jax.nn.silu(mixer_gate_input.astype(jnp.float32))).astype(jnp.bfloat16)
    share_rows = tok_rows // mp_count
    base_output = jnp.einsum(
        "mti,id->tmd", gated_output, shared_output_weight, preferred_element_type=jnp.float32
    )
    low_rank_rows = jnp.dot(
        gated_output[0], adapter_down_weight, preferred_element_type=jnp.float32
    ).astype(jnp.bfloat16)
    adapter_output = jnp.dot(low_rank_rows, adapter_up_weight, preferred_element_type=jnp.float32)
    mixed = lax.psum_scatter(
        jnp.stack([base_output[:, 0] + adapter_output, base_output[:, 1]], axis=1).astype(
            jnp.bfloat16
        ),
        "mp",
        scatter_dimension=0,
        tiled=True,
    ).astype(jnp.float32)
    own_rows = lax.dynamic_slice_in_dim(residual, lax.axis_index("mp") * share_rows, share_rows, 0)
    normed_own = root_norm(own_rows.astype(jnp.float32) + mixed, final_norm_scale)
    normed = lax.all_gather(normed_own, "mp", axis=0, tiled=True)
    vocab_local = vocab_head_weight.shape[1]
    logits = jnp.einsum(
        "tmk,kv->mtv",
        normed,
        lax.all_gather(vocab_head_weight, "seq", axis=0, tiled=True),
        preferred_element_type=jnp.float32,
    )
    vocab_first = lax.axis_index("mp") * vocab_local
    target_hit = (
        scored_token_targets[:, None]
        == vocab_first + jnp.arange(vocab_local, dtype=jnp.int32)[None, :]
    )
    target_local = jnp.sum(jnp.where(target_hit[None], logits, 0.0), axis=2)
    local_max = jnp.max(logits, axis=2)
    vocab_top = lax.pmax(local_max, "mp")
    exp_sums = jnp.sum(jnp.exp(logits - vocab_top[..., None]), axis=2)
    vocab_total, target_logit = lax.psum((exp_sums, target_local), "mp")
    logprob = target_logit - vocab_top - jnp.log(vocab_total)
    token_delta = (logprob[0] - logprob[1]) * valid.astype(jnp.float32)
    roll_sums = jnp.dot(
        token_delta, member_table.astype(jnp.float32), precision=highest
    ) / lengths.astype(jnp.float32)
    owner_rows = (owners[None, :] == jnp.arange(seq_count, dtype=jnp.int32)[:, None]).astype(
        jnp.float32
    ) * roll_sums[None, :]
    owner_sums = lax.psum_scatter(owner_rows, "seq", scatter_dimension=0, tiled=True)
    return (owner_sums, token_delta)


def solution(mesh):
    placed = (
        P("seq"),
        P("seq"),
        P(),
        P(),
        P(),
        P(None, "seq", "mp"),
        P(None, "seq", "mp"),
        P(None, "seq", None),
        P(None, "seq", None),
        P(None, "seq", "mp"),
        P(None, "mp"),
        P(None, "mp"),
        P(None, "seq", "mp", None, None),
        P("mp", None),
        P("mp", None),
        P(),
        P("seq", None, None),
        P(),
        P("seq", "mp"),
    )
    return jax.shard_map(
        shards, mesh=mesh, in_specs=placed, out_specs=(P("seq", None), P("seq")), check_vma=False
    )
```

profile of v0, /device:TPU:0, one launch (start us, length us, event | category | flops | bytes accessed | tf_op | source)
XLA Modules:
  0.0 1076.7 jit_solution(12704770804620089405)
XLA Ops:
  35.8 69.4 %all-gather.4.cloned.1.call-done = bf16[2,32,7,64,64]{4,3,1,2,0:T(8,128)(2,1)} async-done(((bf16[2,1,7,64,64]{4,3,1,2,0:T(8,128)(2,1)}), bf16[2,32,7,64,64]{4,3,1,2,0:T(8,128)(2,1)}) %all-gather.4.cloned.1.call-update) | async-done | bytes 3670032 | tf_op jit(solution)/shard_map/all_gather | solution.py:81
  105.1 7.4 fusion.2
  117.8 498.9 %while.10 = (s32[]{:T(128)}, f32[2,7,64,64]{3,2,1,0:T(8,128)}, f32[2,7]{1,0:T(2,128)S(1)}, f32[2,7,64,64]{3,2,1,0:T(8,128)}, s32[]{:T(128)}) while((s32[]{:T(128)}, f32[2,7,64,64]{3,2,1,0:T(8,128)}, f32[2,7]{1,0:T(2,128)S(1)}, f32[2,7,64,64]{3,2,1,0:T(8,128)}, s32[]{:T(128)}) %tuple.33), condition=%wide.region_7.8_spmd, body=%wide.region_6.7_spmd.sunk | while | flops 114690 | bytes 1605789 | solution.py:102
  122.7 8.9 collective-permute-done
  138.8 7.9 collective-permute-done
  154.0 7.0 collective-permute-done
  215.3 7.3 collective-permute-start
  230.1 7.5 collective-permute-start
  246.0 7.9 collective-permute-start
  253.9 7.5 collective-permute-done
  263.5 8.2 collective-permute-start
  271.7 8.6 collective-permute-done
  282.3 8.2 collective-permute-start
  290.5 9.8 collective-permute-done
  302.3 8.2 collective-permute-start
  310.6 9.9 collective-permute-done
  322.5 7.6 collective-permute-start
  330.1 8.7 collective-permute-done
  347.2 7.4 collective-permute-done
  356.6 7.3 collective-permute-start
  372.5 7.3 collective-permute-start
  387.4 7.3 collective-permute-start
  402.2 7.3 collective-permute-start
  417.1 7.3 collective-permute-start
  431.9 7.3 collective-permute-start
  446.7 7.3 collective-permute-start
  462.2 7.6 collective-permute-start
  469.8 7.1 collective-permute-done
  478.9 8.2 collective-permute-start
  487.1 8.2 collective-permute-done
  497.4 8.2 collective-permute-start
  505.5 9.3 collective-permute-done
  516.9 8.2 collective-permute-start
  525.2 10.3 collective-permute-done
  537.5 7.6 collective-permute-start
  545.1 9.1 collective-permute-done
  556.3 7.1 collective-permute-start
  563.3 8.0 collective-permute-done
  580.2 6.9 collective-permute-done
  589.1 7.3 collective-permute-start
  603.9 7.3 collective-permute-start
  637.7 81.4 %reduce-scatter.2.cloned.1.call-done = bf16[32,2,3584]{2,0,1:T(8,128)(2,1)} async-done(((bf16[256,2,3584]{2,0,1:T(8,128)(2,1)}), bf16[32,2,3584]{2,0,1:T(8,128)(2,1)}) %reduce-scatter.2.cloned.1.call-update) | async-done | bytes 458768 | tf_op jit(solution)/shard_map/reduce_scatter | solution.py:122
  725.4 28.5 %all-gather.6.cloned.1.call-done = bf16[256,2,3584]{2,0,1:T(8,128)(2,1)} async-done(((bf16[32,2,3584]{2,0,1:T(8,128)(2,1)}), bf16[256,2,3584]{2,0,1:T(8,128)(2,1)}) %all-gather.6.cloned.1.call-update) | async-done | bytes 3670032 | tf_op jit(solution)/shard_map/all_gather | solution.py:132
  753.9 132.5 %all-gather.8.cloned.1.call-done = bf16[3584,2000]{1,0:T(8,128)(2,1)} async-done(((bf16[112,2000]{1,0:T(8,128)(2,1)}), bf16[3584,2000]{1,0:T(8,128)(2,1)}) %all-gather.8.cloned.1.call-update) | async-done | bytes 14336016 | tf_op jit(solution)/shard_map/all_gather | solution.py:137
  886.4 13.6 %fusion.6 = (f32[2,256]{1,0:T(2,128)S(1)}, f32[2,256]{1,0:T(2,128)S(1)}, f32[256,2,2000]{0,2,1:T(8,128)}) fusion(pred[256,2000]{0,1:T(8,128)(4,1)} %broadcast_compare_fusion, bf16[256,2,3584]{2,0,1:T(8,128)(2,1)} %all-gather.6.cloned.1.call-done, bf16[3584,2000]{1,0:T(8,128)(2,1)} %all-gather.8.cloned.1.call-done), kind=kOutput, calls=%fused_computation.14 | convolution fusion | flops 7343102976 | bytes 22618112 | tf_op jit(solution)/shard_map/tmk,kv->mtv/dot_general | solution.py:134
  900.0 14.3 %pmax.7 = f32[2,256]{1,0:T(2,128)S(1)} all-reduce(f32[2,256]{1,0:T(2,128)S(1)} %get-tuple-element.26), channel_id=1, replica_groups=mesh['seq'=32,'mp'=8] {'mp'}, use_global_device_ids=true, to_apply=%region_13.14 | all-reduce | flops 512 | bytes 4096 | tf_op jit(solution)/shard_map/pmax | solution.py:147
  917.0 12.4 %all-reduce.1 = (f32[2,256]{1,0:T(2,128)S(1)}, f32[2,256]{1,0:T(2,128)S(1)}) all-reduce(f32[2,256]{1,0:T(2,128)S(1)} %fusion.8, f32[2,256]{1,0:T(2,128)S(1)} %get-tuple-element.25), channel_id=1, replica_groups=mesh['seq'=32,'mp'=8] {'mp'}, use_global_device_ids=true, to_apply=%region_15.16 | all-reduce | flops 1024 | bytes 8192 | tf_op jit(solution)/shard_map/psum | solution.py:149
  929.7 139.3 %all-reduce = f32[32,48]{1,0:T(8,128)S(1)} all-reduce(f32[32,48]{1,0:T(8,128)S(1)} %fusion.54), channel_id=3, replica_groups=mesh['seq'=32,'mp'=8] {'seq'}, use_global_device_ids=true, to_apply=%region_16.17.clone | all-reduce | flops 1536 | bytes 12288
  (173 shorter events, 261.3 us)
Async XLA Ops:
  7.2 613.0 %copy-start = (bf16[448,3584]{1,0:T(8,128)(2,1)S(1)}, bf16[448,3584]{1,0:T(8,128)(2,1)}, u32[]{:S(2)}) copy-start(bf16[448,3584]{1,0:T(8,128)(2,1)} %param.34) | copy-start | bytes 9633796
  7.2 98.0 %all-gather.4.cloned.1.call-start = ((), (), s32[]{:S(2)}) async-start(), calls=%async_computation.1 | async-start | bytes 7569408 | tf_op jit(solution)/shard_map/all_gather | solution.py:81
  7.9 711.1 %reduce-scatter.2.cloned.1.call-start = ((), (), s32[]{:S(2)}) async-start(), calls=%async_computation.2 | async-start | bytes 4128768 | tf_op jit(solution)/shard_map/reduce_scatter | solution.py:122
  30.4 82.1 %copy-start.7 = (bf16[2,256,64]{1,2,0:T(8,128)(2,1)S(1)}, bf16[2,256,64]{1,2,0:T(8,128)(2,1)}, u32[]{:S(2)}) copy-start(bf16[2,256,64]{1,2,0:T(8,128)(2,1)} %param.28) | copy-start | bytes 196612
  105.1 8.8 copy-start.2
  105.1 8.8 copy-start.10
  116.9 499.8 %copy-start.5 = (bf16[2,256,64]{1,2,0:T(8,128)(2,1)S(1)}, bf16[2,256,64]{1,2,0:T(8,128)(2,1)}, u32[]{:S(2)}) copy-start(bf16[2,256,64]{1,2,0:T(8,128)(2,1)} %param.29) | copy-start | bytes 196612
  116.9 499.8 %copy-start.15 = (f32[2,7]{1,0:T(2,128)S(1)}, f32[2,7]{1,0:T(2,128)}, u32[]{:S(2)}) copy-start(f32[2,7]{1,0:T(2,128)} %param.32) | copy-start | bytes 172
  119.8 11.8 %collective-permute-start = (f32[2,7,64,64]{3,2,1,0:T(8,128)}, f32[2,7,64,64]{3,2,1,0:T(8,128)}, u32[]{:S(2)}, u32[]{:S(2)}) collective-permute-start(f32[2,7,64,64]{3,2,1,0:T(8,128)} %multiply_add_fusion.2), channel_id=1, source_target_pairs={{0,8},{8,16},{16,24},{24,32},{32,40},{40,48},{48,56},{56,64},{64,7... | collective-permute-start | bytes 688136 | tf_op jit(solution)/shard_map/while/body/eval_jaxpr/ppermute | solution.py:12
  133.7 13.1 %collective-permute-start = (f32[2,7,64,64]{3,2,1,0:T(8,128)}, f32[2,7,64,64]{3,2,1,0:T(8,128)}, u32[]{:S(2)}, u32[]{:S(2)}) collective-permute-start(f32[2,7,64,64]{3,2,1,0:T(8,128)} %multiply_add_fusion.2), channel_id=1, source_target_pairs={{0,8},{8,16},{16,24},{24,32},{32,40},{40,48},{48,56},{56,64},{64,7... | collective-permute-start | bytes 688136 | tf_op jit(solution)/shard_map/while/body/eval_jaxpr/ppermute | solution.py:12
  148.8 12.2 %collective-permute-start = (f32[2,7,64,64]{3,2,1,0:T(8,128)}, f32[2,7,64,64]{3,2,1,0:T(8,128)}, u32[]{:S(2)}, u32[]{:S(2)}) collective-permute-start(f32[2,7,64,64]{3,2,1,0:T(8,128)} %multiply_add_fusion.2), channel_id=1, source_target_pairs={{0,8},{8,16},{16,24},{24,32},{32,40},{40,48},{48,56},{56,64},{64,7... | collective-permute-start | bytes 688136 | tf_op jit(solution)/shard_map/while/body/eval_jaxpr/ppermute | solution.py:12
  163.1 11.3 %collective-permute-start = (f32[2,7,64,64]{3,2,1,0:T(8,128)}, f32[2,7,64,64]{3,2,1,0:T(8,128)}, u32[]{:S(2)}, u32[]{:S(2)}) collective-permute-start(f32[2,7,64,64]{3,2,1,0:T(8,128)} %multiply_add_fusion.2), channel_id=1, source_target_pairs={{0,8},{8,16},{16,24},{24,32},{32,40},{40,48},{48,56},{56,64},{64,7... | collective-permute-start | bytes 688136 | tf_op jit(solution)/shard_map/while/body/eval_jaxpr/ppermute | solution.py:12
  176.4 10.7 collective-permute-start
  189.1 10.7 collective-permute-start
  201.9 11.4 %collective-permute-start = (f32[2,7,64,64]{3,2,1,0:T(8,128)}, f32[2,7,64,64]{3,2,1,0:T(8,128)}, u32[]{:S(2)}, u32[]{:S(2)}) collective-permute-start(f32[2,7,64,64]{3,2,1,0:T(8,128)} %multiply_add_fusion.2), channel_id=1, source_target_pairs={{0,8},{8,16},{16,24},{24,32},{32,40},{40,48},{48,56},{56,64},{64,7... | collective-permute-start | bytes 688136 | tf_op jit(solution)/shard_map/while/body/eval_jaxpr/ppermute | solution.py:12
  215.3 12.8 %collective-permute-start = (f32[2,7,64,64]{3,2,1,0:T(8,128)}, f32[2,7,64,64]{3,2,1,0:T(8,128)}, u32[]{:S(2)}, u32[]{:S(2)}) collective-permute-start(f32[2,7,64,64]{3,2,1,0:T(8,128)} %multiply_add_fusion.2), channel_id=1, source_target_pairs={{0,8},{8,16},{16,24},{24,32},{32,40},{40,48},{48,56},{56,64},{64,7... | collective-permute-start | bytes 688136 | tf_op jit(solution)/shard_map/while/body/eval_jaxpr/ppermute | solution.py:12
  230.1 13.9 %collective-permute-start = (f32[2,7,64,64]{3,2,1,0:T(8,128)}, f32[2,7,64,64]{3,2,1,0:T(8,128)}, u32[]{:S(2)}, u32[]{:S(2)}) collective-permute-start(f32[2,7,64,64]{3,2,1,0:T(8,128)} %multiply_add_fusion.2), channel_id=1, source_target_pairs={{0,8},{8,16},{16,24},{24,32},{32,40},{40,48},{48,56},{56,64},{64,7... | collective-permute-start | bytes 688136 | tf_op jit(solution)/shard_map/while/body/eval_jaxpr/ppermute | solution.py:12
  246.0 15.4 %collective-permute-start = (f32[2,7,64,64]{3,2,1,0:T(8,128)}, f32[2,7,64,64]{3,2,1,0:T(8,128)}, u32[]{:S(2)}, u32[]{:S(2)}) collective-permute-start(f32[2,7,64,64]{3,2,1,0:T(8,128)} %multiply_add_fusion.2), channel_id=1, source_target_pairs={{0,8},{8,16},{16,24},{24,32},{32,40},{40,48},{48,56},{56,64},{64,7... | collective-permute-start | bytes 688136 | tf_op jit(solution)/shard_map/while/body/eval_jaxpr/ppermute | solution.py:12
  263.5 16.8 %collective-permute-start = (f32[2,7,64,64]{3,2,1,0:T(8,128)}, f32[2,7,64,64]{3,2,1,0:T(8,128)}, u32[]{:S(2)}, u32[]{:S(2)}) collective-permute-start(f32[2,7,64,64]{3,2,1,0:T(8,128)} %multiply_add_fusion.2), channel_id=1, source_target_pairs={{0,8},{8,16},{16,24},{24,32},{32,40},{40,48},{48,56},{56,64},{64,7... | collective-permute-start | bytes 688136 | tf_op jit(solution)/shard_map/while/body/eval_jaxpr/ppermute | solution.py:12
  282.3 18.0 %collective-permute-start = (f32[2,7,64,64]{3,2,1,0:T(8,128)}, f32[2,7,64,64]{3,2,1,0:T(8,128)}, u32[]{:S(2)}, u32[]{:S(2)}) collective-permute-start(f32[2,7,64,64]{3,2,1,0:T(8,128)} %multiply_add_fusion.2), channel_id=1, source_target_pairs={{0,8},{8,16},{16,24},{24,32},{32,40},{40,48},{48,56},{56,64},{64,7... | collective-permute-start | bytes 688136 | tf_op jit(solution)/shard_map/while/body/eval_jaxpr/ppermute | solution.py:12
  302.3 18.1 %collective-permute-start = (f32[2,7,64,64]{3,2,1,0:T(8,128)}, f32[2,7,64,64]{3,2,1,0:T(8,128)}, u32[]{:S(2)}, u32[]{:S(2)}) collective-permute-start(f32[2,7,64,64]{3,2,1,0:T(8,128)} %multiply_add_fusion.2), channel_id=1, source_target_pairs={{0,8},{8,16},{16,24},{24,32},{32,40},{40,48},{48,56},{56,64},{64,7... | collective-permute-start | bytes 688136 | tf_op jit(solution)/shard_map/while/body/eval_jaxpr/ppermute | solution.py:12
  322.5 16.2 %collective-permute-start = (f32[2,7,64,64]{3,2,1,0:T(8,128)}, f32[2,7,64,64]{3,2,1,0:T(8,128)}, u32[]{:S(2)}, u32[]{:S(2)}) collective-permute-start(f32[2,7,64,64]{3,2,1,0:T(8,128)} %multiply_add_fusion.2), channel_id=1, source_target_pairs={{0,8},{8,16},{16,24},{24,32},{32,40},{40,48},{48,56},{56,64},{64,7... | collective-permute-start | bytes 688136 | tf_op jit(solution)/shard_map/while/body/eval_jaxpr/ppermute | solution.py:12
  340.8 13.8 %collective-permute-start = (f32[2,7,64,64]{3,2,1,0:T(8,128)}, f32[2,7,64,64]{3,2,1,0:T(8,128)}, u32[]{:S(2)}, u32[]{:S(2)}) collective-permute-start(f32[2,7,64,64]{3,2,1,0:T(8,128)} %multiply_add_fusion.2), channel_id=1, source_target_pairs={{0,8},{8,16},{16,24},{24,32},{32,40},{40,48},{48,56},{56,64},{64,7... | collective-permute-start | bytes 688136 | tf_op jit(solution)/shard_map/while/body/eval_jaxpr/ppermute | solution.py:12
  356.6 13.8 %collective-permute-start = (f32[2,7,64,64]{3,2,1,0:T(8,128)}, f32[2,7,64,64]{3,2,1,0:T(8,128)}, u32[]{:S(2)}, u32[]{:S(2)}) collective-permute-start(f32[2,7,64,64]{3,2,1,0:T(8,128)} %multiply_add_fusion.2), channel_id=1, source_target_pairs={{0,8},{8,16},{16,24},{24,32},{32,40},{40,48},{48,56},{56,64},{64,7... | collective-permute-start | bytes 688136 | tf_op jit(solution)/shard_map/while/body/eval_jaxpr/ppermute | solution.py:12
  372.5 12.9 %collective-permute-start = (f32[2,7,64,64]{3,2,1,0:T(8,128)}, f32[2,7,64,64]{3,2,1,0:T(8,128)}, u32[]{:S(2)}, u32[]{:S(2)}) collective-permute-start(f32[2,7,64,64]{3,2,1,0:T(8,128)} %multiply_add_fusion.2), channel_id=1, source_target_pairs={{0,8},{8,16},{16,24},{24,32},{32,40},{40,48},{48,56},{56,64},{64,7... | collective-permute-start | bytes 688136 | tf_op jit(solution)/shard_map/while/body/eval_jaxpr/ppermute | solution.py:12
  387.4 12.8 %collective-permute-start = (f32[2,7,64,64]{3,2,1,0:T(8,128)}, f32[2,7,64,64]{3,2,1,0:T(8,128)}, u32[]{:S(2)}, u32[]{:S(2)}) collective-permute-start(f32[2,7,64,64]{3,2,1,0:T(8,128)} %multiply_add_fusion.2), channel_id=1, source_target_pairs={{0,8},{8,16},{16,24},{24,32},{32,40},{40,48},{48,56},{56,64},{64,7... | collective-permute-start | bytes 688136 | tf_op jit(solution)/shard_map/while/body/eval_jaxpr/ppermute | solution.py:12
  402.2 12.8 %collective-permute-start = (f32[2,7,64,64]{3,2,1,0:T(8,128)}, f32[2,7,64,64]{3,2,1,0:T(8,128)}, u32[]{:S(2)}, u32[]{:S(2)}) collective-permute-start(f32[2,7,64,64]{3,2,1,0:T(8,128)} %multiply_add_fusion.2), channel_id=1, source_target_pairs={{0,8},{8,16},{16,24},{24,32},{32,40},{40,48},{48,56},{56,64},{64,7... | collective-permute-start | bytes 688136 | tf_op jit(solution)/shard_map/while/body/eval_jaxpr/ppermute | solution.py:12
  417.1 12.8 %collective-permute-start = (f32[2,7,64,64]{3,2,1,0:T(8,128)}, f32[2,7,64,64]{3,2,1,0:T(8,128)}, u32[]{:S(2)}, u32[]{:S(2)}) collective-permute-start(f32[2,7,64,64]{3,2,1,0:T(8,128)} %multiply_add_fusion.2), channel_id=1, source_target_pairs={{0,8},{8,16},{16,24},{24,32},{32,40},{40,48},{48,56},{56,64},{64,7... | collective-permute-start | bytes 688136 | tf_op jit(solution)/shard_map/while/body/eval_jaxpr/ppermute | solution.py:12
  431.9 12.8 %collective-permute-start = (f32[2,7,64,64]{3,2,1,0:T(8,128)}, f32[2,7,64,64]{3,2,1,0:T(8,128)}, u32[]{:S(2)}, u32[]{:S(2)}) collective-permute-start(f32[2,7,64,64]{3,2,1,0:T(8,128)} %multiply_add_fusion.2), channel_id=1, source_target_pairs={{0,8},{8,16},{16,24},{24,32},{32,40},{40,48},{48,56},{56,64},{64,7... | collective-permute-start | bytes 688136 | tf_op jit(solution)/shard_map/while/body/eval_jaxpr/ppermute | solution.py:12
  446.7 13.4 %collective-permute-start = (f32[2,7,64,64]{3,2,1,0:T(8,128)}, f32[2,7,64,64]{3,2,1,0:T(8,128)}, u32[]{:S(2)}, u32[]{:S(2)}) collective-permute-start(f32[2,7,64,64]{3,2,1,0:T(8,128)} %multiply_add_fusion.2), channel_id=1, source_target_pairs={{0,8},{8,16},{16,24},{24,32},{32,40},{40,48},{48,56},{56,64},{64,7... | collective-permute-start | bytes 688136 | tf_op jit(solution)/shard_map/while/body/eval_jaxpr/ppermute | solution.py:12
  462.2 14.7 %collective-permute-start = (f32[2,7,64,64]{3,2,1,0:T(8,128)}, f32[2,7,64,64]{3,2,1,0:T(8,128)}, u32[]{:S(2)}, u32[]{:S(2)}) collective-permute-start(f32[2,7,64,64]{3,2,1,0:T(8,128)} %multiply_add_fusion.2), channel_id=1, source_target_pairs={{0,8},{8,16},{16,24},{24,32},{32,40},{40,48},{48,56},{56,64},{64,7... | collective-permute-start | bytes 688136 | tf_op jit(solution)/shard_map/while/body/eval_jaxpr/ppermute | solution.py:12
  478.9 16.4 %collective-permute-start = (f32[2,7,64,64]{3,2,1,0:T(8,128)}, f32[2,7,64,64]{3,2,1,0:T(8,128)}, u32[]{:S(2)}, u32[]{:S(2)}) collective-permute-start(f32[2,7,64,64]{3,2,1,0:T(8,128)} %multiply_add_fusion.2), channel_id=1, source_target_pairs={{0,8},{8,16},{16,24},{24,32},{32,40},{40,48},{48,56},{56,64},{64,7... | collective-permute-start | bytes 688136 | tf_op jit(solution)/shard_map/while/body/eval_jaxpr/ppermute | solution.py:12
  497.4 17.5 %collective-permute-start = (f32[2,7,64,64]{3,2,1,0:T(8,128)}, f32[2,7,64,64]{3,2,1,0:T(8,128)}, u32[]{:S(2)}, u32[]{:S(2)}) collective-permute-start(f32[2,7,64,64]{3,2,1,0:T(8,128)} %multiply_add_fusion.2), channel_id=1, source_target_pairs={{0,8},{8,16},{16,24},{24,32},{32,40},{40,48},{48,56},{56,64},{64,7... | collective-permute-start | bytes 688136 | tf_op jit(solution)/shard_map/while/body/eval_jaxpr/ppermute | solution.py:12
  516.9 18.5 %collective-permute-start = (f32[2,7,64,64]{3,2,1,0:T(8,128)}, f32[2,7,64,64]{3,2,1,0:T(8,128)}, u32[]{:S(2)}, u32[]{:S(2)}) collective-permute-start(f32[2,7,64,64]{3,2,1,0:T(8,128)} %multiply_add_fusion.2), channel_id=1, source_target_pairs={{0,8},{8,16},{16,24},{24,32},{32,40},{40,48},{48,56},{56,64},{64,7... | collective-permute-start | bytes 688136 | tf_op jit(solution)/shard_map/while/body/eval_jaxpr/ppermute | solution.py:12
  537.5 16.7 %collective-permute-start = (f32[2,7,64,64]{3,2,1,0:T(8,128)}, f32[2,7,64,64]{3,2,1,0:T(8,128)}, u32[]{:S(2)}, u32[]{:S(2)}) collective-permute-start(f32[2,7,64,64]{3,2,1,0:T(8,128)} %multiply_add_fusion.2), channel_id=1, source_target_pairs={{0,8},{8,16},{16,24},{24,32},{32,40},{40,48},{48,56},{56,64},{64,7... | collective-permute-start | bytes 688136 | tf_op jit(solution)/shard_map/while/body/eval_jaxpr/ppermute | solution.py:12
  556.3 15.0 %collective-permute-start = (f32[2,7,64,64]{3,2,1,0:T(8,128)}, f32[2,7,64,64]{3,2,1,0:T(8,128)}, u32[]{:S(2)}, u32[]{:S(2)}) collective-permute-start(f32[2,7,64,64]{3,2,1,0:T(8,128)} %multiply_add_fusion.2), channel_id=1, source_target_pairs={{0,8},{8,16},{16,24},{24,32},{32,40},{40,48},{48,56},{56,64},{64,7... | collective-permute-start | bytes 688136 | tf_op jit(solution)/shard_map/while/body/eval_jaxpr/ppermute | solution.py:12
  573.3 13.7 %collective-permute-start = (f32[2,7,64,64]{3,2,1,0:T(8,128)}, f32[2,7,64,64]{3,2,1,0:T(8,128)}, u32[]{:S(2)}, u32[]{:S(2)}) collective-permute-start(f32[2,7,64,64]{3,2,1,0:T(8,128)} %multiply_add_fusion.2), channel_id=1, source_target_pairs={{0,8},{8,16},{16,24},{24,32},{32,40},{40,48},{48,56},{56,64},{64,7... | collective-permute-start | bytes 688136 | tf_op jit(solution)/shard_map/while/body/eval_jaxpr/ppermute | solution.py:12
  589.1 12.8 %collective-permute-start = (f32[2,7,64,64]{3,2,1,0:T(8,128)}, f32[2,7,64,64]{3,2,1,0:T(8,128)}, u32[]{:S(2)}, u32[]{:S(2)}) collective-permute-start(f32[2,7,64,64]{3,2,1,0:T(8,128)} %multiply_add_fusion.2), channel_id=1, source_target_pairs={{0,8},{8,16},{16,24},{24,32},{32,40},{40,48},{48,56},{56,64},{64,7... | collective-permute-start | bytes 688136 | tf_op jit(solution)/shard_map/while/body/eval_jaxpr/ppermute | solution.py:12
  603.9 12.8 %collective-permute-start = (f32[2,7,64,64]{3,2,1,0:T(8,128)}, f32[2,7,64,64]{3,2,1,0:T(8,128)}, u32[]{:S(2)}, u32[]{:S(2)}) collective-permute-start(f32[2,7,64,64]{3,2,1,0:T(8,128)} %multiply_add_fusion.2), channel_id=1, source_target_pairs={{0,8},{8,16},{16,24},{24,32},{32,40},{40,48},{48,56},{56,64},{64,7... | collective-permute-start | bytes 688136 | tf_op jit(solution)/shard_map/while/body/eval_jaxpr/ppermute | solution.py:12
  635.5 85.0 %copy-start.9 = (f32[3584]{0:T(1024)S(1)}, f32[3584]{0:T(1024)}, u32[]{:S(2)}) copy-start(f32[3584]{0:T(1024)} %param.38) | copy-start | bytes 43012
  635.5 87.7 %copy-start.18 = (u32[256]{0:T(256)S(1)}, u32[256]{0:T(256)}, u32[]{:S(2)}) copy-start(u32[256]{0:T(256)} %constant.72) | copy-start | bytes 3076
  635.5 88.3 %copy-start.12 = (s32[256]{0:T(256)S(1)}, s32[256]{0:T(256)}, u32[]{:S(2)}) copy-start(s32[256]{0:T(256)} %param.21) | copy-start | bytes 3076
  635.5 118.4 %all-gather.6.cloned.1.call-start = ((), (), s32[]{:S(2)}) async-start(), calls=%async_computation.3 | async-start | bytes 4128768 | tf_op jit(solution)/shard_map/all_gather | solution.py:132
  722.5 163.8 %all-gather.8.cloned.1.call-start = ((), (), s32[]{:S(2)}) async-start(), calls=%async_computation.4 | async-start | bytes 15138816 | tf_op jit(solution)/shard_map/all_gather | solution.py:137
  900.0 29.5 %copy-start.13 = (s32[256]{0:T(256)S(1)}, s32[256]{0:T(256)}, u32[]{:S(2)}) copy-start(s32[256]{0:T(256)} %param.22) | copy-start | bytes 3076
  900.0 29.5 %copy-start.16 = (s32[48]{0:T(128)S(1)}, s32[48]{0:T(128)}, u32[]{:S(2)}) copy-start(s32[48]{0:T(128)} %param.23) | copy-start | bytes 580
  900.0 29.6 %copy-start.17 = (s32[48]{0:T(128)S(1)}, s32[48]{0:T(128)}, u32[]{:S(2)}) copy-start(s32[48]{0:T(128)} %param.24) | copy-start | bytes 580
  929.5 140.7 %copy-start.14 = (f32[256]{0:T(256)}, f32[256]{0:T(256)S(1)}, u32[]{:S(2)}) copy-start(f32[256]{0:T(256)S(1)} %convert_multiply_fusion.4) | copy-start | bytes 3076
  (6 other events, 19.9 us)
Sparse Core Ops, SparseCore 0:
  10.6 94.4 all-gather.3
  635.6 83.3 reduce-scatter.1
  722.7 31.2 all-gather.5
  756.3 129.9 all-gather.7
where the time goes:
time: 1080 us
  waiting for transfers between devices  533 us (49%)
  starting transfers between devices  215 us (20%)
  blocking collectives  166 us (15%)
  other arithmetic  88.2 us (8%)
  matrix products  41 us (4%)
  local copies, waits for them, and re-layouts  18.2 us (2%)
  between operations  14.6 us (1%)
    ppermute x31, waiting for transfers between devices, shifted(): return lax.ppermute(x, axis, pairs)  220 us
    ppermute x31, starting transfers between devices, shifted(): return lax.ppermute(x, axis, pairs)  215 us
    unnamed x1, blocking collectives  139 us
    all_gather x1, waiting for transfers between devices, shards(): lax.all_gather(vocab_head_weight, 'seq', axis=0, tiled=True)  132 us
    reduce_scatter x1, waiting for transfers between devices, shards(): lax.psum_scatter(jnp.stack([base_output[:, 0] + adapter_output, base_outp...  81.4 us
    all_gather x1, waiting for transfers between devices, shards(): piece = lax.all_gather(prompt_held_states, 'seq', axis=1, tiled=True)  69.4 us
    add x31, other arithmetic, relay_step(): outgoing = carry_through[:, :, None, None] * incoming + local_end  63.3 us
    all_gather x1, waiting for transfers between devices, shards(): normed = lax.all_gather(normed_own, 'mp', axis=0, tiled=True)  28.5 us
  transfers between devices with their start and end apart: 35, of which 35 were waited for; matrix products, arithmetic and copies ran while one was open for 3% of the time, Pallas kernels for 0%

commit v1 on v0

v1 whole, which is shorter than its diff:
```python
import functools

import jax
import jax.numpy as jnp
from jax import lax
from jax.experimental import pallas as pl
from jax.experimental.pallas import tpu as pltpu
from jax.sharding import PartitionSpec as P

HIGHEST = lax.Precision.HIGHEST
MESH = pl.DeviceIdType.MESH
Y, Z = 4, 8
X, CORES = 4, 2
REACH = 4
VMEM_BYTES = 56 * 1024 * 1024
LOW = -1e30


def iota(shape, dim):
    return lax.broadcasted_iota(jnp.int32, shape, dim)


def rollout_tables(len_row, first_row, tok):
    lanes = len_row.shape[1]
    row_i, col_i = iota((lanes, lanes), 0), iota((lanes, lanes), 1)
    table = jnp.broadcast_to(len_row, (lanes, lanes))
    starts_col = jnp.sum(jnp.where(col_i < row_i, table, 0.0), axis=1, keepdims=True)
    len_col = jnp.sum(jnp.where(col_i == row_i, table, 0.0), axis=1, keepdims=True)
    starts_row = jnp.sum(jnp.where(row_i < col_i, len_col, 0.0), axis=0, keepdims=True)
    first = jnp.float32(1) * first_row
    pos_col = iota((tok, lanes), 0).astype(jnp.float32) + first
    pos_row = iota((lanes, tok), 1).astype(jnp.float32) + first
    roll_col = jnp.sum(jnp.where(starts_row <= pos_col, 1.0, 0.0), axis=1, keepdims=True) - 1.0
    roll_row = jnp.sum(jnp.where(starts_col <= pos_row, 1.0, 0.0), axis=0, keepdims=True) - 1.0
    return starts_row, roll_col, roll_row, pos_col


def spread(values, heads, inner):
    pick = (iota((heads, inner), 1) // (inner // heads) == iota((heads, inner), 0)).astype(jnp.float32)
    return jnp.dot(values, pick, precision=HIGHEST, preferred_element_type=jnp.float32)


def local_mix_kernel(len_ref, x_ref, b_ref, c_ref, dt_ref, rate_ref, skip_ref, y_ref, dec_ref, e_ref, dl_ref):
    models, tok, inner = x_ref.shape
    heads = dt_ref.shape[2]
    head = inner // heads
    first_row = lax.axis_index("seq") * tok
    _, roll_col, roll_row, _ = rollout_tables(len_ref[...].astype(jnp.float32), first_row, tok)
    t_i, s_i = iota((tok, tok), 0), iota((tok, tok), 1)
    mask = (roll_col == roll_row) & (s_i <= t_i)
    mask_f = mask.astype(jnp.float32)
    tail = roll_col == roll_col[tok - 1 : tok, :]
    eye = (iota((heads, heads), 0) == iota((heads, heads), 1)).astype(jnp.float32)
    for m in range(models):
        dt = dt_ref[m]
        run = jnp.dot(mask_f, -dt * rate_ref[m : m + 1, :], precision=HIGHEST, preferred_element_type=jnp.float32)
        up = jnp.log(dt) - run
        up_rows = lax.dot_general(
            eye, up, (((1,), (1,)), ((), ())), precision=HIGHEST, preferred_element_type=jnp.float32
        )
        gram = lax.dot_general(
            c_ref[m], b_ref[m], (((1,), (1,)), ((), ())), preferred_element_type=jnp.float32
        )
        x_f = x_ref[m].astype(jnp.float32)
        pair = 2 * head
        skips = spread(jnp.broadcast_to(skip_ref[m : m + 1, :], (8, heads)), heads, inner)[0:1]
        for lo in range(0, inner, pair):
            width = min(pair, inner - lo)
            x_pair = x_ref[m, :, lo : lo + width]
            outs = []
            for h in range(lo // head, (lo + width) // head):
                gap = jnp.where(mask, run[:, h : h + 1] + up_rows[h : h + 1, :], LOW)
                weights = (jnp.exp(gap) * gram).astype(jnp.bfloat16)
                outs.append(jnp.dot(weights, x_pair, preferred_element_type=jnp.float32))
            part = outs[0]
            if len(outs) == 2:
                part = jnp.where(iota((tok, width), 1) < head, outs[0], outs[1])
            y_ref[m, :, lo : lo + width] = part + skips[:, lo : lo + width] * x_f[:, lo : lo + width]
        last = run[tok - 1 : tok, :]
        end_w = jnp.where(tail, jnp.exp(jnp.where(tail, last + up, LOW)), 0.0)
        x_end = (x_f * spread(end_w, heads, inner)).astype(jnp.bfloat16)
        e_ref[m] = lax.dot_general(
            b_ref[m], x_end, (((0,), (0,)), ((), ())), preferred_element_type=jnp.float32
        ).astype(jnp.bfloat16)
        dl_ref[m] = spread(jnp.broadcast_to(last, (8, heads)), heads, inner)
        dec_ref[m] = spread(jnp.exp(run), heads, inner)


def vmem():
    return pl.BlockSpec(memory_space=pltpu.VMEM)


def anywhere():
    return pl.BlockSpec(memory_space=pl.ANY)


def smem():
    return pl.BlockSpec(memory_space=pltpu.SMEM)


def local_mix(len_row, x, b, c, dt, rate, skip):
    models, tok, inner = x.shape
    state = b.shape[2]
    return pl.pallas_call(
        local_mix_kernel,
        out_shape=(
            jax.ShapeDtypeStruct((models, tok, inner), jnp.float32),
            jax.ShapeDtypeStruct((models, tok, inner), jnp.float32),
            jax.ShapeDtypeStruct((models, state, inner), jnp.bfloat16),
            jax.ShapeDtypeStruct((models, 8, inner), jnp.float32),
        ),
        in_specs=[vmem()] * 7,
        out_specs=(vmem(),) * 4,
        compiler_params=pltpu.CompilerParams(vmem_limit_bytes=VMEM_BYTES),
        cost_estimate=pl.CostEstimate(flops=2 * 10**9, bytes_accessed=4 * 10**6, transcendentals=10**6),
        name="local_mix",
    )(len_row, x, b, c, dt, rate, skip)


def greet(barrier, peers):
    for peer in peers:
        pl.semaphore_signal(barrier, inc=1, device_id=peer, device_id_type=MESH)
    pl.semaphore_wait(barrier, len(peers))


def states_kernel(
    pt_ref, e_ref, dl_ref, wo_ref, dw_ref,
    pall_ref, en_ref, dn_ref, wos_ref, dws_ref,
    send_sem, recv_sem, send2, recv2, own_sem,
):
    seq, mp = lax.axis_index("seq"), lax.axis_index("mp")
    z, y = seq // Y, lax.rem(seq, Y)
    count = Y * Z

    def at_y(d):
        return (z * Y + lax.rem(y + d + Y, Y), mp)

    def at_z(d):
        return (lax.rem(z + d + Z, Z) * Y + y, mp)

    def at_s(d):
        return (lax.rem(seq + d + count, count), mp)

    sibling = (seq, mp + 1 - 2 * lax.rem(mp, CORES))
    greet(
        pltpu.get_barrier_semaphore(),
        [at_y(1), at_y(-1), at_y(2), at_z(1), at_z(-1), sibling]
        + [at_s(d) for d in range(1, REACH + 1)]
        + [at_s(-d) for d in range(1, REACH + 1)],
    )
    slot = [0]

    def send(src, dst, peer):
        k = slot[0]
        slot[0] += 1
        copy = pltpu.make_async_remote_copy(
            src_ref=src, dst_ref=dst, send_sem=send_sem.at[k], recv_sem=recv_sem.at[k],
            device_id=peer, device_id_type=MESH,
        )
        copy.start()
        return copy

    own = [
        pltpu.make_async_copy(pt_ref.at[m], pall_ref.at[m, z, y], own_sem.at[m]) for m in range(2)
    ]
    for copy in own:
        copy.start()
    waits = []
    a_y = [send(pt_ref.at[0], pall_ref.at[0, z, y], at_y(d)) for d in (1, -1, 2)]
    b_right = send(pt_ref.at[1], pall_ref.at[1, z, y], at_z(1))
    b_left = send(pt_ref.at[1], pall_ref.at[1, z, y], at_z(-1))
    for d in range(1, REACH + 1):
        waits.append(send(e_ref, en_ref.at[d - 1], at_s(d)))
        waits.append(send(dl_ref, dn_ref.at[d - 1], at_s(d)))
    waits.append(send(wo_ref, wos_ref, sibling))
    waits.append(send(dw_ref, dws_ref, sibling))
    for copy in own:
        copy.wait()
    for copy in a_y:
        copy.wait_recv()
    a_right = send(pall_ref.at[0, z], pall_ref.at[0, z], at_z(1))
    a_left = send(pall_ref.at[0, z], pall_ref.at[0, z], at_z(-1))
    sends = list(a_y) + [b_right, b_left, a_right, a_left]
    for k in range(1, Z // 2):
        src = lax.rem(z - k + Z, Z)
        b_right.wait_recv()
        b_right = send(pall_ref.at[1, src, y], pall_ref.at[1, src, y], at_z(1))
        sends.append(b_right)
        src = lax.rem(z + k, Z)
        b_left.wait_recv()
        if k < Z // 2 - 1:
            b_left = send(pall_ref.at[1, src, y], pall_ref.at[1, src, y], at_z(-1))
            sends.append(b_left)
    b_right.wait_recv()
    b_y = [send(pall_ref.at[1, :, y], pall_ref.at[1, :, y], at_y(d)) for d in (1, -1, 2)]
    for k in range(1, Z // 2):
        src = lax.rem(z - k + Z, Z)
        a_right.wait_recv()
        a_right = send(pall_ref.at[0, src], pall_ref.at[0, src], at_z(1))
        sends.append(a_right)
        src = lax.rem(z + k, Z)
        a_left.wait_recv()
        if k < Z // 2 - 1:
            a_left = send(pall_ref.at[0, src], pall_ref.at[0, src], at_z(-1))
            sends.append(a_left)
    a_right.wait_recv()
    for copy in b_y:
        copy.wait_recv()
    for copy in waits:
        copy.wait_recv()
    for copy in sends + b_y + waits:
        copy.wait_send()


def states(pt, e, dl, wo, dw):
    models, state, inner = pt.shape
    out = (
        jax.ShapeDtypeStruct((models, Z, Y, state, inner), pt.dtype),
        jax.ShapeDtypeStruct((REACH,) + e.shape, e.dtype),
        jax.ShapeDtypeStruct((REACH,) + dl.shape, dl.dtype),
        jax.ShapeDtypeStruct(wo.shape, wo.dtype),
        jax.ShapeDtypeStruct(dw.shape, dw.dtype),
    )
    copies = 3 + 2 * REACH + 2 + 3 + 2 * 7
    return pl.pallas_call(
        states_kernel,
        out_shape=out,
        in_specs=[anywhere()] * 5,
        out_specs=(anywhere(),) * 5,
        scratch_shapes=[
            pltpu.SemaphoreType.DMA((copies,)),
            pltpu.SemaphoreType.DMA((copies,)),
            pltpu.SemaphoreType.DMA((1,)),
            pltpu.SemaphoreType.DMA((1,)),
            pltpu.SemaphoreType.DMA((2,)),
        ],
        compiler_params=pltpu.CompilerParams(
            collective_id=1, has_side_effects=True, vmem_limit_bytes=VMEM_BYTES
        ),
        cost_estimate=pl.CostEstimate(flops=0, bytes_accessed=10**8, transcendentals=0),
        name="state_exchange",
    )(pt, e, dl, wo, dw)


def finish_mix_kernel(
    len_s, hold_s, len_ref, hold_ref, y_ref, dec_ref, c_ref, z_ref, pall_ref, en_ref, dn_ref, g_ref, acc_ref
):
    models, tok, inner = y_ref.shape
    first_row = lax.axis_index("seq") * tok
    starts_row, roll_col, _, _ = rollout_tables(len_ref[...].astype(jnp.float32), first_row, tok)
    first = jnp.float32(1) * first_row
    start0 = jnp.max(jnp.where(starts_row <= first, starts_row, -1.0), axis=1, keepdims=True)
    inherits = start0 < first
    fresh_rows = jnp.where(starts_row < first, 1.0, 0.0)
    lanes = starts_row.shape[1]
    lane_f = iota((tok, lanes), 1).astype(jnp.float32)
    inherited = jnp.sum(jnp.where(roll_col == lane_f, fresh_rows, 0.0), axis=1, keepdims=True) > 0.5

    def scan(r, carry):
        start, lo, hi, hold0 = carry
        lo = jnp.where(start < first_row, r + 1, lo)
        hi = jnp.where(start < first_row + tok, r + 1, hi)
        hold0 = jnp.where(start < first_row, hold_s[0, r], hold0)
        return start + len_s[0, r], lo, hi, hold0

    rolls = len_s.shape[1]
    _, lo, hi, hold0 = lax.fori_loop(
        0, rolls, scan, (jnp.int32(0), jnp.int32(0), jnp.int32(0), jnp.int32(-1))
    )
    hold0 = jnp.where(hold0 < 0, -1, hold0)
    source = jnp.maximum(hold0, 0)
    for m in range(models):
        total = jnp.zeros((1, inner), jnp.float32)
        arriving = jnp.zeros((c_ref.shape[2], inner), jnp.float32)
        for k in range(1, REACH + 1):
            near = start0 < first - jnp.float32((k - 1) * tok)
            arriving = arriving + jnp.where(near, jnp.exp(total) * en_ref[k - 1, m].astype(jnp.float32), 0.0)
            total = jnp.where(near, total + dn_ref[k - 1, m][0:1], total)
        begun = jnp.exp(total) * pall_ref[m, source].astype(jnp.float32)
        arriving = arriving + jnp.where(inherits & (hold0 >= 0), begun, 0.0)
        c_in = jnp.where(inherited, c_ref[m].astype(jnp.float32), 0.0).astype(jnp.bfloat16)
        high = arriving.astype(jnp.bfloat16)
        low = (arriving - high.astype(jnp.float32)).astype(jnp.bfloat16)
        acc_ref[m] = jnp.dot(c_in, high, preferred_element_type=jnp.float32) + jnp.dot(
            c_in, low, preferred_element_type=jnp.float32
        )

    def borrow(r, carry):
        held = hold_s[0, r]

        @pl.when(held >= 0)
        def _():
            mine = roll_col == r.astype(jnp.float32)
            for m in range(models):
                c_r = jnp.where(mine, c_ref[m].astype(jnp.float32), 0.0).astype(jnp.bfloat16)
                acc_ref[m] += jnp.dot(c_r, pall_ref[m, held], preferred_element_type=jnp.float32)

        return carry

    lax.fori_loop(lo, hi, borrow, 0)
    for m in range(models):
        gate = z_ref[m].astype(jnp.float32)
        out = y_ref[m] + dec_ref[m] * acc_ref[m]
        g_ref[m] = (out * (gate / (1.0 + jnp.exp(-gate)))).astype(jnp.bfloat16)


def finish_mix(len_row, hold_row, lengths, holders, y, dec, c, z, pall, en, dn):
    models, tok, inner = y.shape
    return pl.pallas_call(
        finish_mix_kernel,
        out_shape=jax.ShapeDtypeStruct((models, tok, inner), jnp.bfloat16),
        in_specs=[smem()] * 2 + [vmem()] * 9,
        out_specs=vmem(),
        scratch_shapes=[pltpu.VMEM((models, tok, inner), jnp.float32)],
        compiler_params=pltpu.CompilerParams(vmem_limit_bytes=VMEM_BYTES),
        cost_estimate=pl.CostEstimate(flops=10**9, bytes_accessed=8 * 10**6, transcendentals=10**6),
        name="finish_mix",
    )(lengths, holders, len_row, hold_row, y, dec, c, z, pall, en, dn)


def project_kernel(
    g_ref, wo_ref, wos_ref, dw_ref, dws_ref, up_ref, res_ref, scale_ref, nall_ref,
    gs_ref, low_ref, acc_ref, out_ref, in_ref, h_ref, n_ref,
    g_send, g_recv, r_send, r_recv, a_send, a_recv, f_send, f_recv, own_sem,
):
    seq, mp = lax.axis_index("seq"), lax.axis_index("mp")
    x, core = mp // CORES, lax.rem(mp, CORES)
    chunks = acc_ref.shape[0]
    width = acc_ref.shape[4]
    share = res_ref.shape[1]
    model_width = res_ref.shape[2]
    inner = g_ref.shape[4]
    rows = X * share
    sibling = (seq, x * CORES + 1 - core)

    def at_x(d):
        return (seq, lax.rem(x + d + X, X) * CORES + core)

    greet(pltpu.get_barrier_semaphore(), [sibling, at_x(1), at_x(2), at_x(3)])
    gated = pltpu.make_async_remote_copy(
        src_ref=g_ref.at[:, :, 1 - core], dst_ref=gs_ref, send_sem=g_send, recv_sem=g_recv,
        device_id=sibling, device_id_type=MESH,
    )
    gated.start()
    own_g = g_ref[:, :, core].reshape(2 * rows, inner)
    low = jnp.dot(own_g[:rows], dw_ref[...], preferred_element_type=jnp.float32)
    gated.wait_recv()
    sib_g = gs_ref[...].reshape(2 * rows, inner)
    low = low + jnp.dot(sib_g[:rows], dws_ref[...], preferred_element_type=jnp.float32)
    low_ref[...] = low.astype(jnp.bfloat16)

    def scatter(n, d):
        return pltpu.make_async_remote_copy(
            src_ref=out_ref.at[n, :, lax.rem(x + d, X)], dst_ref=in_ref.at[d - 1, n],
            send_sem=r_send.at[d - 1, n], recv_sem=r_recv.at[d - 1, n],
            device_id=at_x(d), device_id_type=MESH,
        )

    def chunk(n, carry):
        cols = pl.ds(pl.multiple_of(n * width, width), width)
        acc = jnp.dot(
            g_ref[:, :, core].reshape(2 * rows, inner), wo_ref[:, cols], preferred_element_type=jnp.float32
        ) + jnp.dot(gs_ref[...].reshape(2 * rows, inner), wos_ref[:, cols], preferred_element_type=jnp.float32)
        more = jnp.dot(low_ref[...], up_ref[:, cols], preferred_element_type=jnp.float32)
        acc_ref[n, 0] = (acc[:rows] + more).reshape(X, share, width)
        acc_ref[n, 1] = acc[rows:].reshape(X, share, width)
        out_ref[n] = acc_ref[n].astype(jnp.bfloat16)
        for d in (2, 1, 3):
            scatter(n, d).start()
        return carry

    lax.fori_loop(0, chunks, chunk, 0)

    def gather(n, square):
        cols = pl.ds(pl.multiple_of(n * width, width), width)
        total = acc_ref[n, :, x]
        for d in (1, 3, 2):
            scatter(n, d).wait_recv()
            total = total + in_ref[d - 1, n].astype(jnp.float32)
        total = total + res_ref[:, :, cols].astype(jnp.float32)
        h_ref[:, :, cols] = total
        return square + jnp.sum(total * total, axis=2, keepdims=True)

    square = lax.fori_loop(0, chunks, gather, jnp.zeros((2, share, 1), jnp.float32))
    n_ref[...] = (h_ref[...] * lax.rsqrt(square / model_width + 1e-05) * scale_ref[...]).astype(jnp.bfloat16)

    def spread_out(m, d):
        return pltpu.make_async_remote_copy(
            src_ref=n_ref.at[m], dst_ref=nall_ref.at[m, mp],
            send_sem=a_send.at[d, m], recv_sem=a_recv.at[d, m],
            device_id=sibling if d == 0 else at_x(d), device_id_type=MESH,
        )

    def forward(m, d):
        block = nall_ref.at[m, lax.rem(x - d + X, X) * CORES + core]
        return pltpu.make_async_remote_copy(
            src_ref=block, dst_ref=block, send_sem=f_send.at[d - 1, m], recv_sem=f_recv.at[d - 1, m],
            device_id=sibling, device_id_type=MESH,
        )

    for m in range(2):
        for d in (2, 1, 3, 0):
            spread_out(m, d).start()
    keep = pltpu.make_async_copy(n_ref, nall_ref.at[:, mp], own_sem)
    keep.start()
    for m in range(2):
        for d in (1, 3, 2):
            spread_out(m, d).wait_recv()
            forward(m, d).start()
    keep.wait()
    gated.wait_send()

    def drain(n, carry):
        for d in (1, 2, 3):
            scatter(n, d).wait_send()
        return carry

    lax.fori_loop(0, chunks, drain, 0)
    for m in range(2):
        spread_out(m, 0).wait_recv()
        for d in range(4):
            spread_out(m, d).wait_send()
        for d in (1, 2, 3):
            forward(m, d).wait_send()
            forward(m, d).wait_recv()


def project(gated, wo, wos, dw, dws, up, res, scale):
    models, tok, inner = gated.shape
    width_all = wo.shape[1]
    share = res.shape[1]
    width = 512
    chunks = width_all // width
    bf16, f32 = jnp.bfloat16, jnp.float32
    dma = pltpu.SemaphoreType.DMA
    return pl.pallas_call(
        project_kernel,
        out_shape=jax.ShapeDtypeStruct((models, X * CORES, share, width_all), bf16),
        in_specs=[vmem()] * 8,
        out_specs=anywhere(),
        scratch_shapes=[
            pltpu.VMEM((models, X, share, inner), bf16),
            pltpu.VMEM((X * share, dw.shape[1]), bf16),
            pltpu.VMEM((chunks, models, X, share, width), f32),
            pltpu.VMEM((chunks, models, X, share, width), bf16),
            pltpu.VMEM((X - 1, chunks, models, share, width), bf16),
            pltpu.VMEM((models, share, width_all), f32),
            pltpu.VMEM((models, share, width_all), bf16),
            dma, dma, dma((3, chunks)), dma((3, chunks)), dma((4, 2)), dma((4, 2)), dma((3, 2)), dma((3, 2)), dma,
        ],
        compiler_params=pltpu.CompilerParams(
            collective_id=2, has_side_effects=True, vmem_limit_bytes=VMEM_BYTES
        ),
        cost_estimate=pl.CostEstimate(flops=10**10, bytes_accessed=10**8, transcendentals=0),
        name="project_norm",
    )(gated.reshape(models, X, CORES, share, inner), wo, wos, dw, dws, up, res, scale)


def logits_kernel(vocab, n_ref, w_ref, tgt_ref, stat_ref, max_ref, sum_ref, hit_ref):
    step = pl.program_id(0)
    tile = w_ref.shape[1]
    rows = n_ref.shape[0]

    @pl.when(step == 0)
    def _():
        max_ref[...] = jnp.full(max_ref.shape, -3e38, jnp.float32)
        sum_ref[...] = jnp.zeros(sum_ref.shape, jnp.float32)
        hit_ref[...] = jnp.zeros(hit_ref.shape, jnp.float32)

    logits = jnp.dot(n_ref[...], w_ref[...], preferred_element_type=jnp.float32)
    col = iota((rows, tile), 1) + step * tile
    real = col < vocab
    logits = jnp.where(real, logits, -3e38)
    top = jnp.maximum(max_ref[...], jnp.max(logits, axis=1, keepdims=True))
    sum_ref[...] = sum_ref[...] * jnp.exp(max_ref[...] - top) + jnp.sum(
        jnp.where(real, jnp.exp(logits - top), 0.0), axis=1, keepdims=True
    )
    max_ref[...] = top
    hit_ref[...] += jnp.sum(jnp.where(real & (col == tgt_ref[...]), logits, 0.0), axis=1, keepdims=True)

    @pl.when(step == pl.num_programs(0) - 1)
    def _():
        lane = iota((rows, 128), 1)
        packed = jnp.where(
            lane == 0, max_ref[...], jnp.where(lane == 1, sum_ref[...], jnp.where(lane == 2, hit_ref[...], 0.0))
        )
        stat_ref[...] = jnp.transpose(packed)[0:8]


def logit_stats(normed, weight, target):
    rows, depth = normed.shape
    vocab = weight.shape[1]
    tile = 512
    return pl.pallas_call(
        functools.partial(logits_kernel, vocab),
        grid=(pl.cdiv(vocab, tile),),
        out_shape=jax.ShapeDtypeStruct((8, rows), jnp.float32),
        in_specs=[
            pl.BlockSpec((rows, depth), lambda j: (0, 0), pipeline_mode=pl.Buffered(1)),
            pl.BlockSpec((depth, tile), lambda j: (0, j)),
            pl.BlockSpec((rows, 1), lambda j: (0, 0), pipeline_mode=pl.Buffered(1)),
        ],
        out_specs=pl.BlockSpec((8, rows), lambda j: (0, 0)),
        scratch_shapes=[pltpu.VMEM((rows, 1), jnp.float32)] * 3,
        compiler_params=pltpu.CompilerParams(vmem_limit_bytes=VMEM_BYTES),
        cost_estimate=pl.CostEstimate(flops=8 * 10**9, bytes_accessed=2 * 10**7, transcendentals=10**6),
        name="logit_stats",
    )(normed, weight, target)


def deltas_kernel(
    stat_ref, valid_ref, len_ref, owner_ref, sums_ref, delta_ref,
    all_ref, part_ref, parts_ref, s_send, s_recv, p_send, p_recv,
):
    seq, mp = lax.axis_index("seq"), lax.axis_index("mp")
    peers, count = X * CORES, Y * Z
    tok = valid_ref.shape[1]
    barrier = pltpu.get_barrier_semaphore()
    for d in range(1, peers):
        pl.semaphore_signal(barrier, inc=1, device_id=(seq, lax.rem(mp + d, peers)), device_id_type=MESH)

    def hello(d, carry):
        pl.semaphore_signal(barrier, inc=1, device_id=(lax.rem(seq + d, count), mp), device_id_type=MESH)
        return carry

    lax.fori_loop(1, count, hello, 0)
    pl.semaphore_wait(barrier, peers - 1 + count - 1)

    def stats(d):
        return pltpu.make_async_remote_copy(
            src_ref=stat_ref, dst_ref=all_ref.at[mp], send_sem=s_send.at[d], recv_sem=s_recv.at[d],
            device_id=(seq, lax.rem(mp + d, peers)), device_id_type=MESH,
        )

    for d in range(1, peers):
        stats(d).start()
    all_ref[mp] = stat_ref[...]
    starts_row, roll_col, _, _ = rollout_tables(len_ref[...].astype(jnp.float32), seq * tok, tok)
    lanes = starts_row.shape[1]
    member = (roll_col == iota((tok, lanes), 1).astype(jnp.float32)).astype(jnp.float32)
    for d in range(1, peers):
        stats(d).wait_recv()
    tops = [all_ref[k][0:1] for k in range(peers)]
    top = functools.reduce(jnp.maximum, tops)
    total = functools.reduce(
        jnp.add, [all_ref[k][1:2] * jnp.exp(tops[k] - top) for k in range(peers)]
    )
    hit = functools.reduce(jnp.add, [all_ref[k][2:3] for k in range(peers)])
    logprob = hit - top - jnp.log(total)
    delta = (logprob[:, :tok] - logprob[:, tok:]) * valid_ref[...].astype(jnp.float32)
    delta_ref[...] = delta
    part_ref[...] = jnp.dot(
        jnp.broadcast_to(delta, (8, tok)), member, precision=HIGHEST, preferred_element_type=jnp.float32
    )

    def parts(d):
        return pltpu.make_async_remote_copy(
            src_ref=part_ref, dst_ref=parts_ref.at[seq], send_sem=p_send.at[d], recv_sem=p_recv.at[d],
            device_id=(lax.rem(seq + d, count), mp), device_id_type=MESH,
        )

    def begin(d, carry):
        parts(d).start()
        return carry

    def end(d, carry):
        parts(d).wait_recv()
        return carry

    def drain(d, carry):
        parts(d).wait_send()
        return carry

    lax.fori_loop(1, count, begin, 0)
    parts_ref[seq] = part_ref[...]
    lax.fori_loop(1, count, end, 0)
    sums = functools.reduce(jnp.add, [parts_ref[k] for k in range(count)])[0:1] / len_ref[...].astype(jnp.float32)
    mine = jnp.where(owner_ref[...] == seq, sums, 0.0)
    sums_ref[...] = mine[:, : sums_ref.shape[1]]
    for d in range(1, peers):
        stats(d).wait_send()
    lax.fori_loop(1, count, drain, 0)


def deltas(stat, valid_row, len_row, owner_row, rolls):
    peers, count = X * CORES, Y * Z
    tok = valid_row.shape[1]
    lanes = len_row.shape[1]
    dma = pltpu.SemaphoreType.DMA
    return pl.pallas_call(
        deltas_kernel,
        out_shape=(
            jax.ShapeDtypeStruct((1, rolls), jnp.float32),
            jax.ShapeDtypeStruct((1, tok), jnp.float32),
        ),
        in_specs=[vmem()] * 4,
        out_specs=(vmem(),) * 2,
        scratch_shapes=[
            pltpu.VMEM((peers,) + stat.shape, jnp.float32),
            pltpu.VMEM((8, lanes), jnp.float32),
            pltpu.VMEM((count, 8, lanes), jnp.float32),
            dma((peers,)), dma((peers,)), dma((count,)), dma((count,)),
        ],
        compiler_params=pltpu.CompilerParams(
            collective_id=3, has_side_effects=True, vmem_limit_bytes=VMEM_BYTES
        ),
        name="deltas",
    )(stat, valid_row, len_row, owner_row)


def shards(
    scored_token_targets, valid, lengths, owners, holders, mixer_input_x, mixer_gate_input,
    input_projection_b, output_projection_c, token_step_sizes, head_decay_rate, head_skip_scale,
    prompt_held_states, shared_output_weight, adapter_down_weight, adapter_up_weight,
    residual, final_norm_scale, vocab_head_weight,
):
    tok = scored_token_targets.shape[0]
    models, _, inner = mixer_input_x.shape
    state = input_projection_b.shape[2]
    rolls = lengths.shape[0]
    share = tok // (X * CORES)
    mp = lax.axis_index("mp")
    head_all = lax.all_gather(vocab_head_weight, "seq", axis=0, tiled=True)

    def row(values, fill):
        return jnp.pad(values, (0, 128 - rolls), constant_values=fill)[None, :]

    len_row, hold_row, owner_row = row(lengths, 0), row(holders, -1), row(owners, -1)
    prompts = jnp.transpose(prompt_held_states[:, 0], (0, 3, 1, 2)).reshape(models, state, inner)
    own_res = jnp.transpose(lax.dynamic_slice_in_dim(residual, mp * share, share, 0), (1, 0, 2))
    y, dec, ends, last = local_mix(
        len_row, mixer_input_x, input_projection_b, output_projection_c, token_step_sizes,
        head_decay_rate, head_skip_scale,
    )
    pall, en, dn, wos, dws = states(prompts, ends, last, shared_output_weight, adapter_down_weight)
    gated = finish_mix(
        len_row, hold_row, lengths[None, :], holders[None, :], y, dec, output_projection_c, mixer_gate_input,
        pall.reshape(models, Z * Y, state, inner), en, dn,
    )
    normed = project(
        gated, shared_output_weight, wos, adapter_down_weight, dws, adapter_up_weight, own_res,
        final_norm_scale[None, :],
    )
    vocab = vocab_head_weight.shape[1]
    local = scored_token_targets - mp * vocab
    target = jnp.concatenate([local, local])[:, None]
    stat = logit_stats(normed.reshape(models * tok, -1), head_all, target)
    sums, delta = deltas(stat, valid[None, :], len_row, owner_row, rolls)
    return sums, delta.reshape(tok)


def solution(mesh):
    placed = (
        P("seq"), P("seq"), P(), P(), P(),
        P(None, "seq", "mp"), P(None, "seq", "mp"),
        P(None, "seq", None), P(None, "seq", None), P(None, "seq", "mp"),
        P(None, "mp"), P(None, "mp"), P(None, "seq", "mp", None, None),
        P("mp", None), P("mp", None), P(), P("seq", None, None), P(), P("seq", "mp"),
    )
    return jax.shard_map(
        shards, mesh=mesh, in_specs=placed, out_specs=(P("seq", None), P("seq")), check_vma=False
    )
```

time: 1080 us -> 237 us (0.22)
  waiting for transfers between devices: 533 us -> 0.7 us
  starting transfers between devices: 215 us -> 0.04 us
  Pallas kernels: 0 us -> 202 us
  blocking collectives: 166 us -> 0 us
  other arithmetic: 88.2 us -> 0.01 us
  matrix products: 41 us -> 0 us
    all_gather x3 -> x1, waiting for transfers between devices: 230 us -> 0.02 us  [shards(): head_all = lax.all_gather(vocab_head_weight, 'seq', axis=0, tiled=True)]
    ppermute x31 -> x0, waiting for transfers between devices: 220 us -> none  [shifted(): return lax.ppermute(x, axis, pairs)]
    ppermute x31 -> x0, starting transfers between devices: 215 us -> none  [shifted(): return lax.ppermute(x, axis, pairs)]
    pallas_call x0 -> x6, Pallas kernels: none -> 202 us  [the longest x1 94.9 us: states(): pl.pallas_call(states_kernel, out_shape=out, in_specs=[anywhere()] * 5, o...]
    unnamed x1 -> x0, blocking collectives: 139 us -> none
    reduce_scatter x1 -> x0, waiting for transfers between devices: 81.4 us -> none  [shards(): lax.psum_scatter(jnp.stack([base_output[:, 0] + adapter_output, base_outp...]
    add x33 -> x0, other arithmetic: 63.3 us -> none  [the longest x31 63.3 us: relay_step(): outgoing = carry_through[:, :, None, None] * incoming + local_end]
    dot_general x10 -> x0, matrix products: 41 us -> none  [the longest x1 13.6 us: shards(): jnp.einsum('tmk,kv->mtv', normed, lax.all_gather(vocab_head_weight, 'seq'...]
  transfers between devices with their start and end apart: 35 -> 1, of which waited for: 35 -> 0; matrix products, arithmetic and copies ran while one was open for 3% -> 6% of each run, Pallas kernels for 0% -> 70%
where the time goes in v1:
time: 237 us; the launch traced here: 235 us
  Pallas kernels  202 us (85%)
  local copies, waits for them, and re-layouts  17.6 us (7%)
  between operations  14.1 us (6%)
    pallas_call x1, Pallas kernels, states(): pl.pallas_call(states_kernel, out_shape=out, in_specs=[anywhere()] * 5, o...  94.9 us
    pallas_call x1, Pallas kernels, project(): pl.pallas_call(project_kernel, out_shape=jax.ShapeDtypeStruct((models, X...  54.9 us
    pallas_call x1, Pallas kernels, deltas(): pl.pallas_call(deltas_kernel, out_shape=(jax.ShapeDtypeStruct((1, rolls),...  21.7 us
    pallas_call x1, Pallas kernels, logit_stats(): pl.pallas_call(functools.partial(logits_kernel, vocab), grid=(pl.cdiv(voc...  16.3 us
    unnamed x18, local copies, waits for them, and re-layouts  12 us
    pallas_call x1, Pallas kernels, local_mix(): pl.pallas_call(local_mix_kernel, out_shape=(jax.ShapeDtypeStruct((models,...  7.46 us
    pallas_call x1, Pallas kernels, finish_mix(): pl.pallas_call(finish_mix_kernel, out_shape=jax.ShapeDtypeStruct((models,...  6.86 us
  transfers between devices with their start and end apart: 1, of which 0 were waited for; matrix products, arithmetic and copies ran while one was open for 6% of the time, Pallas kernels for 70%

profile of v1, /device:TPU:0, one launch (start us, length us, event | category | flops | bytes accessed | tf_op | source)
XLA Modules:
  0.0 234.5 jit_solution(7606272743870106925)
XLA Ops:
  7.2 0.0 copy-start
  7.2 0.0 copy-start.2
  7.2 0.0 copy-start.1
  7.2 0.0 copy-start.4
  7.2 0.0 all-gather.2.cloned.1.call-start
  7.3 0.7 all-gather.2.cloned.1.call-update
  7.9 1.6 copy.31.c_ref
  9.5 2.0 copy.29.x_ref
  11.6 1.6 copy.32.dt_ref
  13.1 1.6 copy.30.b_ref
  14.7 1.7 copy.38.pt_ref
  16.4 2.0 copy.35.z_ref
  18.5 1.3 constant_dynamic-slice_fusion
  19.8 0.8 copy.41
  20.6 0.0 copy-done
  20.6 0.6 broadcast_in_dim.28.scale_ref
  21.2 0.0 copy-done.2
  21.3 0.9 copy.37.tgt_ref
  22.1 0.0 copy-done.1
  22.1 0.0 copy-done.4
  22.1 0.5 pad_bitcast_fusion
  22.6 0.0 copy-start.3
  22.6 7.5 %local_mix.1 = (f32[2,256,448]{2,1,0:T(8,128)}, f32[2,256,448]{2,1,0:T(8,128)}, bf16[2,64,448]{2,1,0:T(8,128)(2,1)}, f32[2,8,448]{2,1,0:T(8,128)}) custom-call(s32[1,128]{1,0:T(1,128)} %get-tuple-element.25.len_ref, bf16[2,256,448]{2,1,0:T(8,128)(2,1)} %copy.29.x_ref, bf16[2,256,64]{2,1,0:T(8,128)(2,1)} %copy.30.b_ref, bf16[2,256,64]{2,1,0:T(8,128)(2,1)} %copy.31.c_ref, ...), custom_call_target="tpu_custom_call" | custom-call | flops 2000000000 | bytes 4000000 | tf_op jit(solution)/shard_map/local_mix/pallas_call | solution.py:104
  30.1 94.9 %state_exchange.1 = (bf16[2,8,4,64,448]{4,3,2,1,0:T(8,128)(2,1)}, bf16[4,2,64,448]{3,2,1,0:T(8,128)(2,1)}, f32[4,2,8,448]{3,2,1,0:T(8,128)}, bf16[448,3584]{1,0:T(8,128)(2,1)}, bf16[448,128]{1,0:T(8,128)(2,1)}) custom-call(bf16[2,64,448]{2,1,0:T(8,128)(2,1)} %copy.38.pt_ref, bf16[2,64,448]{2,1,0:T(8,128)(2,1)} %get-tuple-element.15.e_ref, ...), custom_call_target="tpu_custom_call" | custom-call | bytes 100000000 | tf_op jit(solution)/shard_map/state_exchange/pallas_call | solution.py:225
  125.0 0.0 copy-done.3
  125.0 0.5 pad_bitcast_fusion.1.hold_ref
  125.5 6.9 %finish_mix.1 = bf16[2,256,448]{2,1,0:T(8,128)(2,1)} custom-call(s32[1,48]{1,0:T(1,128)} %bitcast.27, s32[1,48]{1,0:T(1,128)} %bitcast.30, s32[1,128]{1,0:T(1,128)} %get-tuple-element.25.len_ref, s32[1,128]{1,0:T(1,128)} %pad_bitcast_fusion.1.hold_ref, f32[2,256,448]{2,1,0:T(8,128)} %get-tuple-element.13.y_ref, f32[2,256,448]{2,1,0:T(8,128)} %get-tuple-element.14.dec_ref, ...), custom_call_target="tpu_custom_call" | custom-call | flops 1000000000 | bytes 8000000 | tf_op jit(solution)/shard_map/finish_mix/pallas_call | solution.py:309
  132.4 54.9 %project_norm.1 = bf16[2,8,32,3584]{3,2,1,0:T(8,128)(2,1)} custom-call(bf16[2,4,2,32,448]{4,3,2,1,0:T(8,128)(2,1)} %bitcast.23, bf16[448,3584]{1,0:T(8,128)(2,1)} %wo_ref.3, bf16[448,3584]{1,0:T(8,128)(2,1)} %get-tuple-element.20.wos_ref, bf16[448,128]{1,0:T(8,128)(2,1)} %dw_ref.3, bf16[448,128]{1,0:T(8,128)(2,1)} %get-tuple-element.21.dws_ref, ...), custom_call_target="tpu_custom_call" | custom-call | flops 10000000000 | bytes 100000000 | tf_op jit(solution)/shard_map/project_norm/pallas_call | solution.py:436
  187.3 0.0 all-gather.2.cloned.1.call-done.w_ref
  187.3 16.3 %logit_stats.1.stat_ref = f32[8,512]{1,0:T(8,128)} custom-call(bf16[512,3584]{1,0:T(8,128)(2,1)} %bitcast.31, bf16[3584,2000]{1,0:T(8,128)(2,1)} %all-gather.2.cloned.1.call-done.w_ref, s32[512,1]{1,0:T(8,128)} %copy.37.tgt_ref), custom_call_target="tpu_custom_call" | custom-call | flops 8000000000 | bytes 20000000 | tf_op jit(solution)/shard_map/logit_stats/pallas_call | solution.py:494
  203.7 21.7 %deltas.1 = (f32[1,48]{1,0:T(1,128)}, f32[1,256]{1,0:T(1,128)}) custom-call(f32[8,512]{1,0:T(8,128)} %logit_stats.1.stat_ref, s32[1,256]{1,0:T(1,128)} %bitcast.28, s32[1,128]{1,0:T(1,128)} %get-tuple-element.25.len_ref, s32[1,128]{1,0:T(1,128)} %get-tuple-element.24.owner_ref), custom_call_target="tpu_custom_call" | custom-call | tf_op jit(solution)/shard_map/deltas/pallas_call | solution.py:590
  225.3 1.1 copy.44
  226.4 1.2 copy.45
  (2 shorter events, 0.0 us)
Async XLA Ops:
  7.2 13.5 %copy-start = (f32[3584]{0:T(1024)S(1)}, f32[3584]{0:T(1024)}, u32[]{:S(2)}) copy-start(f32[3584]{0:T(1024)} %param.36) | copy-start | bytes 43012
  7.2 14.1 %copy-start.2 = (s32[256]{0:T(256)S(1)}, s32[256]{0:T(256)}, u32[]{:S(2)}) copy-start(s32[256]{0:T(256)} %param.19) | copy-start | bytes 3076
  7.2 14.9 %copy-start.1 = (s32[48]{0:T(128)S(1)}, s32[48]{0:T(128)}, u32[]{:S(2)}) copy-start(s32[48]{0:T(128)} %param.21) | copy-start | bytes 580
  7.2 14.9 %copy-start.4 = (s32[48]{0:T(128)S(1)}, s32[48]{0:T(128)}, u32[]{:S(2)}) copy-start(s32[48]{0:T(128)} %param.22) | copy-start | bytes 580
  7.2 180.1 %all-gather.2.cloned.1.call-start = ((), (), s32[]{:S(2)}) async-start(), calls=%async_computation | async-start | bytes 15138816 | tf_op jit(solution)/shard_map/all_gather | solution.py:623
  22.6 102.3 %copy-start.3 = (s32[48]{0:T(128)S(1)}, s32[48]{0:T(128)}, u32[]{:S(2)}) copy-start(s32[48]{0:T(128)} %param.23) | copy-start | bytes 580
Sparse Core Ops, SparseCore 0:
  10.6 159.3 all-gather.1

commit v2 on v1

v2 whole, which is shorter than its diff:
```python
import functools

import jax
import jax.numpy as jnp
from jax import lax
from jax.experimental import pallas as pl
from jax.experimental.pallas import tpu as pltpu
from jax.sharding import PartitionSpec as P

HIGHEST = lax.Precision.HIGHEST
MESH = pl.DeviceIdType.MESH
Y, Z = 4, 8
X, CORES = 4, 2
REACH = 4
VMEM_BYTES = 56 * 1024 * 1024
LOW = -1e30


def iota(shape, dim):
    return lax.broadcasted_iota(jnp.int32, shape, dim)


def rollout_tables(len_row, first_row, tok):
    lanes = len_row.shape[1]
    row_i, col_i = iota((lanes, lanes), 0), iota((lanes, lanes), 1)
    table = jnp.broadcast_to(len_row, (lanes, lanes))
    starts_col = jnp.sum(jnp.where(col_i < row_i, table, 0.0), axis=1, keepdims=True)
    len_col = jnp.sum(jnp.where(col_i == row_i, table, 0.0), axis=1, keepdims=True)
    starts_row = jnp.sum(jnp.where(row_i < col_i, len_col, 0.0), axis=0, keepdims=True)
    first = jnp.float32(1) * first_row
    pos_col = iota((tok, lanes), 0).astype(jnp.float32) + first
    pos_row = iota((lanes, tok), 1).astype(jnp.float32) + first
    roll_col = jnp.sum(jnp.where(starts_row <= pos_col, 1.0, 0.0), axis=1, keepdims=True) - 1.0
    roll_row = jnp.sum(jnp.where(starts_col <= pos_row, 1.0, 0.0), axis=0, keepdims=True) - 1.0
    return starts_row, roll_col, roll_row, pos_col


def local_mix_kernel(len_ref, x_ref, b_ref, c_ref, dt_ref, rate_ref, skip_ref, y_ref, run_ref, e_ref, dl_ref, xw_ref):
    models, inner, tok = x_ref.shape
    heads = dt_ref.shape[0]
    head = inner // heads
    state = b_ref.shape[1]
    first_row = lax.axis_index("seq") * tok
    _, roll_col, roll_row, _ = rollout_tables(len_ref[...].astype(jnp.float32), first_row, tok)
    s_i, t_i = iota((tok, tok), 0), iota((tok, tok), 1)
    mask = (roll_col == roll_row) & (s_i <= t_i)
    mask_f = mask.astype(jnp.float32)
    eye = (s_i == t_i).astype(jnp.float32)
    tail = roll_row == roll_row[:, tok - 1 : tok]
    lasts = []
    for m in range(models):
        dt = dt_ref[:, m, :]
        heads_eye = iota((heads, heads), 0) == iota((heads, heads), 1)
        rate = jnp.sum(jnp.where(heads_eye, rate_ref[m : m + 1, :], 0.0), axis=1, keepdims=True)
        run = jnp.dot(-dt * rate, mask_f, precision=HIGHEST, preferred_element_type=jnp.float32)
        up = jnp.log(dt) - run
        up_cols = lax.dot_general(
            eye, up, (((1,), (1,)), ((), ())), precision=HIGHEST, preferred_element_type=jnp.float32
        )
        gram = lax.dot_general(
            b_ref[m], c_ref[m], (((0,), (0,)), ((), ())), preferred_element_type=jnp.float32
        )
        last = run[:, tok - 1 : tok]
        end_w = jnp.where(tail, jnp.exp(jnp.where(tail, last + up, LOW)), 0.0)
        for h in range(heads):
            rows = slice(h * head, (h + 1) * head)
            gap = jnp.where(mask, run[h : h + 1, :] + up_cols[:, h : h + 1], LOW)
            weights = (jnp.exp(gap) * gram).astype(jnp.bfloat16)
            x_h = x_ref[m, rows, :]
            x_f = x_h.astype(jnp.float32)
            y_ref[m, rows, :] = (
                jnp.dot(x_h, weights, preferred_element_type=jnp.float32) + skip_ref[m, h] * x_f
            )
            xw_ref[rows, :] = (x_f * end_w[h : h + 1, :]).astype(jnp.bfloat16)
        e_ref[:, m * state : (m + 1) * state] = lax.dot_general(
            xw_ref[...], b_ref[m], (((1,), (1,)), ((), ())), preferred_element_type=jnp.float32
        ).astype(jnp.bfloat16)
        run_ref[m, 0:heads, :] = run
        lasts.append(last)
    dl_ref[...] = jnp.zeros(dl_ref.shape, jnp.float32)
    dl_ref[0:heads, :] = jnp.where(iota((heads, models * state), 1) < state, lasts[0], lasts[1])


def vmem():
    return pl.BlockSpec(memory_space=pltpu.VMEM)


def anywhere():
    return pl.BlockSpec(memory_space=pl.ANY)


def smem():
    return pl.BlockSpec(memory_space=pltpu.SMEM)


def local_mix(len_row, x, b, c, dt, rate, skip):
    models, inner, tok = x.shape
    state = b.shape[1]
    return pl.pallas_call(
        local_mix_kernel,
        out_shape=(
            jax.ShapeDtypeStruct((models, inner, tok), jnp.float32),
            jax.ShapeDtypeStruct((models, 8, tok), jnp.float32),
            jax.ShapeDtypeStruct((inner, models * state), jnp.bfloat16),
            jax.ShapeDtypeStruct((8, models * state), jnp.float32),
        ),
        in_specs=[vmem()] * 6 + [smem()],
        out_specs=(vmem(),) * 4,
        scratch_shapes=[pltpu.VMEM((inner, tok), jnp.bfloat16)],
        compiler_params=pltpu.CompilerParams(vmem_limit_bytes=VMEM_BYTES),
        cost_estimate=pl.CostEstimate(flops=2 * 10**9, bytes_accessed=4 * 10**6, transcendentals=10**6),
        name="local_mix",
    )(len_row, x, b, c, dt, rate, skip)


def greet(barrier, peers):
    for peer in peers:
        pl.semaphore_signal(barrier, inc=1, device_id=peer, device_id_type=MESH)
    pl.semaphore_wait(barrier, len(peers))


def make_sender(send_sem, recv_sem):
    taken, begun = [0], []

    def send(src, dst, peer):
        k = taken[0]
        taken[0] += 1
        copy = pltpu.make_async_remote_copy(
            src_ref=src, dst_ref=dst, send_sem=send_sem.at[k], recv_sem=recv_sem.at[k],
            device_id=peer, device_id_type=MESH,
        )
        copy.start()
        begun.append(copy)
        return copy

    return send, begun


RING_COPIES = 3 + 2 + 2 + 8 + 8 + 16 + 16


def place():
    seq, mp = lax.axis_index("seq"), lax.axis_index("mp")
    z, y = seq // Y, lax.rem(seq, Y)

    def at_y(d):
        return (z * Y + lax.rem(y + d + Y, Y), mp)

    def at_z(d):
        return (lax.rem(z + d + Z, Z) * Y + y, mp)

    return seq, mp, z, y, at_y, at_z


def torus_ring(send, own_ref, all_ref, split, own_sem):
    _, _, z, y, at_y, at_z = place()
    rows = own_ref.shape[0]
    half = (rows - split) // 2
    first, second = pl.ds(0, split), pl.ds(split, rows - split)
    low, high = pl.ds(split, half), pl.ds(split + half, rows - split - half)

    def zz(d):
        return lax.rem(z + d + Z, Z)

    def yy(d):
        return lax.rem(y + d + Y, Y)

    def along(ref, peer):
        return send(ref, ref, peer)

    pending, last = [], []

    def to_y(d):
        src = all_ref.at[zz(d), y, second] if d else own_ref.at[second]
        dst = all_ref.at[zz(d), y, second]
        pending.append((zz(d), send(src, dst, at_y(1)), send(src, dst, at_y(-1))))

    def pass_y():
        j, up, down = pending.pop(0)
        up.wait_recv()
        last.append(along(all_ref.at[j, yy(-1), low], at_y(1)))
        down.wait_recv()
        last.append(along(all_ref.at[j, yy(1), high], at_y(-1)))

    keep = pltpu.make_async_copy(own_ref, all_ref.at[z, y], own_sem)
    keep.start()
    firsts = [send(own_ref.at[first], all_ref.at[z, y, first], at_y(d)) for d in (1, -1, 2)]
    right = send(own_ref.at[second], all_ref.at[z, y, second], at_z(1))
    left = send(own_ref.at[second], all_ref.at[z, y, second], at_z(-1))
    to_y(0)
    keep.wait()
    yield
    for copy in firsts:
        copy.wait_recv()
    group = all_ref.at[z, :, first]
    far_right, far_left = along(group, at_z(1)), along(group, at_z(-1))
    yield
    for k in range(1, Z // 2):
        right.wait_recv()
        right = along(all_ref.at[zz(-k), y, second if k < Z // 2 - 1 else low], at_z(1))
        to_y(-k)
        left.wait_recv()
        left = along(all_ref.at[zz(k), y, second if k < Z // 2 - 1 else high], at_z(-1))
        to_y(k)
        yield
        pass_y()
        yield
        if k > 1:
            far_right.wait_recv()
            far_right = along(all_ref.at[zz(1 - k), :, first], at_z(1))
            far_left.wait_recv()
            far_left = along(all_ref.at[zz(k - 1), :, first], at_z(-1))
            yield
    right.wait_recv()
    left.wait_recv()
    to_y(Z // 2)
    yield
    pass_y()
    pass_y()
    yield
    far_right.wait_recv()
    far_right = along(all_ref.at[zz(1 - Z // 2), pl.ds(0, Y // 2), first], at_z(1))
    far_left.wait_recv()
    far_left = along(all_ref.at[zz(Z // 2 - 1), pl.ds(Y // 2, Y // 2), first], at_z(-1))
    yield
    while pending:
        pass_y()
        yield
    far_right.wait_recv()
    far_left.wait_recv()
    for copy in last:
        copy.wait_recv()


def states_kernel(
    pt_ref, e_ref, dl_ref, wo_ref, dw_ref,
    pall_ref, en_ref, dn_ref, wos_ref, dws_ref,
    send_sem, recv_sem, own_sem,
):
    seq, mp, _, _, at_y, at_z = place()
    count = Y * Z

    def at_s(d):
        return (lax.rem(seq + d + count, count), mp)

    sibling = (seq, mp + 1 - 2 * lax.rem(mp, CORES))
    greet(
        pltpu.get_barrier_semaphore(),
        [at_y(1), at_y(-1), at_y(2), at_z(1), at_z(-1), sibling]
        + [at_s(d) for d in range(1, REACH + 1)]
        + [at_s(-d) for d in range(1, REACH + 1)],
    )
    send, begun = make_sender(send_sem, recv_sem)
    ring = torus_ring(send, pt_ref, pall_ref, PROMPT_SPLIT, own_sem)
    next(ring)
    waits = []
    for d in range(1, REACH + 1):
        waits.append(send(e_ref, en_ref.at[d - 1], at_s(d)))
        waits.append(send(dl_ref, dn_ref.at[d - 1], at_s(d)))
    waits.append(send(wo_ref, wos_ref, sibling))
    waits.append(send(dw_ref, dws_ref, sibling))
    for _ in ring:
        pass
    for copy in waits:
        copy.wait_recv()
    for copy in begun:
        copy.wait_send()


PROMPT_SPLIT = 192
HEAD_SPLIT = 48
HEAD_NATIVE = 1024
TILE = 256


def states(pt, e, dl, wo, dw):
    out = (
        jax.ShapeDtypeStruct((Z, Y) + pt.shape, pt.dtype),
        jax.ShapeDtypeStruct((REACH,) + e.shape, e.dtype),
        jax.ShapeDtypeStruct((REACH,) + dl.shape, dl.dtype),
        jax.ShapeDtypeStruct(wo.shape, wo.dtype),
        jax.ShapeDtypeStruct(dw.shape, dw.dtype),
    )
    copies = RING_COPIES + 2 * REACH + 2
    return pl.pallas_call(
        states_kernel,
        out_shape=out,
        in_specs=[anywhere()] * 5,
        out_specs=(anywhere(),) * 5,
        scratch_shapes=[
            pltpu.SemaphoreType.DMA((copies,)),
            pltpu.SemaphoreType.DMA((copies,)),
            pltpu.SemaphoreType.DMA,
        ],
        compiler_params=pltpu.CompilerParams(
            collective_id=1, has_side_effects=True, vmem_limit_bytes=VMEM_BYTES
        ),
        cost_estimate=pl.CostEstimate(flops=0, bytes_accessed=10**8, transcendentals=0),
        name="state_exchange",
    )(pt, e, dl, wo, dw)


def finish_mix_kernel(
    len_s, hold_s, len_ref, y_ref, run_ref, c_ref, z_ref, pall_ref, en_ref, dn_ref, g_ref, acc_ref
):
    models, inner, tok = y_ref.shape
    lanes_all = pall_ref.shape[2]
    head = lanes_all // models
    heads = inner // head
    first_row = lax.axis_index("seq") * tok
    starts_row, _, roll_row, _ = rollout_tables(len_ref[...].astype(jnp.float32), first_row, tok)
    first = jnp.float32(1) * first_row
    start0 = jnp.max(jnp.where(starts_row <= first, starts_row, -1.0), axis=1, keepdims=True)
    inherits = start0 < first
    roll0 = jnp.where(inherits, roll_row[:, 0:1], -1.0)
    inherited = roll_row == roll0

    def scan(r, carry):
        start, lo, hi, hold0 = carry
        lo = jnp.where(start < first_row, r + 1, lo)
        hi = jnp.where(start < first_row + tok, r + 1, hi)
        hold0 = jnp.where(start < first_row, hold_s[0, r], hold0)
        return start + len_s[0, r], lo, hi, hold0

    rolls = len_s.shape[1]
    _, lo, hi, hold0 = lax.fori_loop(
        0, rolls, scan, (jnp.int32(0), jnp.int32(0), jnp.int32(0), jnp.int32(-1))
    )
    hold0 = jnp.where(hold0 < 0, -1, hold0)
    source = jnp.maximum(hold0, 0)
    arriving = []
    for h in range(heads):
        rows = slice(h * head, (h + 1) * head)
        total = jnp.zeros((1, lanes_all), jnp.float32)
        part = jnp.zeros((head, lanes_all), jnp.float32)
        for k in range(1, REACH + 1):
            near = start0 < first - jnp.float32((k - 1) * tok)
            part = part + jnp.where(near, jnp.exp(total) * en_ref[k - 1, rows, :].astype(jnp.float32), 0.0)
            total = jnp.where(near, total + dn_ref[k - 1, h : h + 1, :], total)
        begun = jnp.exp(total) * pall_ref[source, rows, :].astype(jnp.float32)
        arriving.append(part + jnp.where(inherits & (hold0 >= 0), begun, 0.0))
    arriving = jnp.concatenate(arriving, axis=0)
    high = arriving.astype(jnp.bfloat16)
    low = (arriving - high.astype(jnp.float32)).astype(jnp.bfloat16)
    c_all = jnp.concatenate([c_ref[m].astype(jnp.float32) for m in range(models)], axis=0)
    of_model = iota((lanes_all, tok), 0) // c_ref.shape[1]

    def masked(tokens, m):
        return jnp.where(tokens & (of_model == m), c_all, 0.0).astype(jnp.bfloat16)

    for m in range(models):
        c_in = masked(inherited, m)
        acc_ref[m] = jnp.dot(high, c_in, preferred_element_type=jnp.float32) + jnp.dot(
            low, c_in, preferred_element_type=jnp.float32
        )

    def borrow(r, carry):
        held = hold_s[0, r]

        @pl.when(held >= 0)
        def _():
            mine = roll_row == r.astype(jnp.float32)
            for m in range(models):
                acc_ref[m] += jnp.dot(pall_ref[held], masked(mine, m), preferred_element_type=jnp.float32)

        return carry

    lax.fori_loop(lo, hi, borrow, 0)
    for m in range(models):
        for h in range(heads):
            rows = slice(h * head, (h + 1) * head)
            gate = z_ref[m, rows, :].astype(jnp.float32)
            out = y_ref[m, rows, :] + jnp.exp(run_ref[m, h : h + 1, :]) * acc_ref[m, rows, :]
            acc_ref[m, rows, :] = out * (gate / (1.0 + jnp.exp(-gate)))
        g_ref[m] = jnp.transpose(acc_ref[m]).astype(jnp.bfloat16)


def finish_mix(len_row, lengths, holders, y, run, c, z, pall, en, dn):
    models, inner, tok = y.shape
    return pl.pallas_call(
        finish_mix_kernel,
        out_shape=jax.ShapeDtypeStruct((models, tok, inner), jnp.bfloat16),
        in_specs=[smem()] * 2 + [vmem()] * 8,
        out_specs=vmem(),
        scratch_shapes=[pltpu.VMEM((models, inner, tok), jnp.float32)],
        compiler_params=pltpu.CompilerParams(vmem_limit_bytes=VMEM_BYTES),
        cost_estimate=pl.CostEstimate(flops=10**9, bytes_accessed=8 * 10**6, transcendentals=10**6),
        name="finish_mix",
    )(lengths, holders, len_row, y, run, c, z, pall, en, dn)


def project_kernel(
    g_ref, wo_ref, wos_ref, dw_ref, dws_ref, up_ref, res_ref, scale_ref, head_ref, nall_ref, wall_ref,
    gs_ref, low_ref, acc_ref, out_ref, comb_ref, relay_ref, direct_ref, sum_ref, h_ref, n_ref,
    send_sem, recv_sem, ring_send, ring_recv, own_sem, keep_sem,
):
    seq, mp, _, _, at_y, at_z = place()
    x, core = mp // CORES, lax.rem(mp, CORES)
    chunks = acc_ref.shape[0]
    width = acc_ref.shape[4]
    share = res_ref.shape[1]
    model_width = res_ref.shape[2]
    inner = g_ref.shape[4]
    rows = X * share
    sibling = (seq, x * CORES + 1 - core)

    def xx(d):
        return lax.rem(x + d + X, X)

    def at_x(d):
        return (seq, xx(d) * CORES + core)

    greet(
        pltpu.get_barrier_semaphore(),
        [sibling, at_x(1), at_x(-1), at_y(1), at_y(-1), at_y(2), at_z(1), at_z(-1)],
    )
    send, begun = make_sender(send_sem, recv_sem)
    ring_out, ring_begun = make_sender(ring_send, ring_recv)
    gated = send(g_ref.at[:, :, 1 - core], gs_ref, sibling)
    ring = torus_ring(ring_out, head_ref, wall_ref, HEAD_SPLIT, own_sem)

    def ring_step(times=1):
        for _ in range(times):
            next(ring, None)

    ring_step()
    own_g = g_ref[:, :, core].reshape(2 * rows, inner)
    low = jnp.dot(own_g[:rows], dw_ref[...], preferred_element_type=jnp.float32)
    gated.wait_recv()
    sib_g = gs_ref[...].reshape(2 * rows, inner)
    low = low + jnp.dot(sib_g[:rows], dws_ref[...], preferred_element_type=jnp.float32)
    low_ref[...] = low.astype(jnp.bfloat16)

    relays, directs, sums = [], [], []

    def combine(n):
        for side, d, m in ((0, 1, 0), (1, -1, 1)):
            relays[n][side].wait_recv()
            total = acc_ref[n, m, xx(d)] + relay_ref[n, side].astype(jnp.float32)
            comb_ref[n, side] = total.astype(jnp.bfloat16)
        sums.append(
            [send(comb_ref.at[n, side], sum_ref.at[n, side], at_x(d)) for side, d in ((0, 1), (1, -1))]
        )

    for n in range(chunks):
        cols = slice(n * width, (n + 1) * width)
        acc = jnp.dot(
            g_ref[:, :, core].reshape(2 * rows, inner), wo_ref[:, cols], preferred_element_type=jnp.float32
        ) + jnp.dot(gs_ref[...].reshape(2 * rows, inner), wos_ref[:, cols], preferred_element_type=jnp.float32)
        more = jnp.dot(low_ref[...], up_ref[:, cols], preferred_element_type=jnp.float32)
        acc_ref[n, 0] = (acc[:rows] + more).reshape(X, share, width)
        acc_ref[n, 1] = acc[rows:].reshape(X, share, width)
        out_ref[n] = acc_ref[n].astype(jnp.bfloat16)
        far = xx(2)
        relays.append(
            [send(out_ref.at[n, m, far], relay_ref.at[n, side], at_x(d)) for side, d, m in ((0, 1, 0), (1, -1, 1))]
        )
        directs.append(
            [
                send(out_ref.at[n, m, xx(d)], direct_ref.at[n, side], at_x(d))
                for side, d, m in ((0, 1, 1), (1, -1, 0))
            ]
        )
        if n >= 1:
            combine(n - 1)
        if n in (1, 3, 5):
            ring_step()
    combine(chunks - 1)
    ring_step()

    square = jnp.zeros((2, share, 1), jnp.float32)
    for n in range(chunks):
        cols = slice(n * width, (n + 1) * width)
        for copy in sums[n] + directs[n]:
            copy.wait_recv()
        squares = []
        for m in range(2):
            total = (
                acc_ref[n, m, x]
                + sum_ref[n, m].astype(jnp.float32)
                + direct_ref[n, 1 - m].astype(jnp.float32)
                + res_ref[m, :, cols].astype(jnp.float32)
            )
            h_ref[m, :, cols] = total
            squares.append(jnp.sum(total * total, axis=1, keepdims=True))
        square = square + jnp.stack(squares)
        if n in (1, 3, 5):
            ring_step()
    n_ref[...] = (h_ref[...] * lax.rsqrt(square / model_width + 1e-05) * scale_ref[...]).astype(jnp.bfloat16)

    def block(d, m):
        return nall_ref.at[m, xx(d) * CORES + core]

    near = [[None, None], [None, None]]
    for side, d, m in ((0, 1, 0), (1, -1, 1), (0, 1, 1), (1, -1, 0)):
        near[side][m] = send(n_ref.at[m], block(0, m), at_x(d))
    shared = [send(n_ref.at[m], block(0, m), sibling) for m in range(2)]
    keep = pltpu.make_async_copy(n_ref, nall_ref.at[:, mp], keep_sem)
    keep.start()
    ring_step()
    far = []
    for side, d, m in ((0, 1, 0), (1, -1, 1)):
        near[side][m].wait_recv()
        far.append(send(block(-d, m), block(-d, m), at_x(d)))
        shared.append(send(block(-d, m), block(-d, m), sibling))
    ring_step(2)
    for side, d, m in ((0, 1, 1), (1, -1, 0)):
        near[side][m].wait_recv()
        shared.append(send(block(-d, m), block(-d, m), sibling))
    ring_step(2)
    for side, m in ((0, 0), (1, 1)):
        far[side].wait_recv()
        shared.append(send(block(2, m), block(2, m), sibling))
    for _ in ring:
        pass
    keep.wait()
    for copy in shared:
        copy.wait_recv()
    for copy in begun + ring_begun:
        copy.wait_send()


def project(gated, wo, wos, dw, dws, up, res, scale, head):
    models, tok, inner = gated.shape
    width_all = wo.shape[1]
    share = res.shape[1]
    width = 512
    chunks = width_all // width
    bf16, f32 = jnp.bfloat16, jnp.float32
    dma = pltpu.SemaphoreType.DMA
    copies = 1 + 6 * chunks + 4 + 2 + 2 + 6
    piece = pltpu.VMEM((chunks, 2, share, width), bf16)
    return pl.pallas_call(
        project_kernel,
        out_shape=(
            jax.ShapeDtypeStruct((models, X * CORES, share, width_all), bf16),
            jax.ShapeDtypeStruct((Z, Y) + head.shape, bf16),
        ),
        in_specs=[vmem()] * 8 + [anywhere()],
        out_specs=(anywhere(),) * 2,
        scratch_shapes=[
            pltpu.VMEM((models, X, share, inner), bf16),
            pltpu.VMEM((X * share, dw.shape[1]), bf16),
            pltpu.VMEM((chunks, models, X, share, width), f32),
            pltpu.VMEM((chunks, models, X, share, width), bf16),
            piece, piece, piece, piece,
            pltpu.VMEM((models, share, width_all), f32),
            pltpu.VMEM((models, share, width_all), bf16),
            dma((copies,)), dma((copies,)), dma((RING_COPIES,)), dma((RING_COPIES,)), dma, dma,
        ],
        compiler_params=pltpu.CompilerParams(
            collective_id=2, has_side_effects=True, vmem_limit_bytes=VMEM_BYTES
        ),
        cost_estimate=pl.CostEstimate(flops=10**10, bytes_accessed=10**8, transcendentals=0),
        name="project_norm",
    )(gated.reshape(models, X, CORES, share, inner), wo, wos, dw, dws, up, res, scale, head)


def scores_kernel(
    vocab, native, n_ref, w1_ref, w2_ref, tgt_ref, valid_ref, len_ref, owner_ref, sums_ref, delta_ref,
    max_ref, sum_ref, hit_ref, stat_ref, all_ref, part_ref, parts_ref, s_send, s_recv, p_send, p_recv,
):
    seq, mp = lax.axis_index("seq"), lax.axis_index("mp")
    peers, count = X * CORES, Y * Z
    step = pl.program_id(0)
    tile = w1_ref.shape[1]
    rows = n_ref.shape[0]
    barrier = pltpu.get_barrier_semaphore()

    @pl.when(step == 0)
    def _():
        for d in range(1, peers):
            pl.semaphore_signal(barrier, inc=1, device_id=(seq, lax.rem(mp + d, peers)), device_id_type=MESH)

        def hello(d, carry):
            pl.semaphore_signal(barrier, inc=1, device_id=(lax.rem(seq + d, count), mp), device_id_type=MESH)
            return carry

        lax.fori_loop(1, count, hello, 0)
        max_ref[...] = jnp.full(max_ref.shape, -3e38, jnp.float32)
        sum_ref[...] = jnp.zeros(sum_ref.shape, jnp.float32)
        hit_ref[...] = jnp.zeros(hit_ref.shape, jnp.float32)

    def add(w_ref):
        logits = jnp.dot(n_ref[...], w_ref[...], preferred_element_type=jnp.float32)
        col = iota((rows, tile), 1) + step * tile
        real = col < vocab
        logits = jnp.where(real, logits, -3e38)
        top = jnp.maximum(max_ref[...], jnp.max(logits, axis=1, keepdims=True))
        sum_ref[...] = sum_ref[...] * jnp.exp(max_ref[...] - top) + jnp.sum(
            jnp.where(real, jnp.exp(logits - top), 0.0), axis=1, keepdims=True
        )
        max_ref[...] = top
        hit_ref[...] += jnp.sum(jnp.where(real & (col == tgt_ref[...]), logits, 0.0), axis=1, keepdims=True)

    @pl.when(step < native)
    def _():
        add(w1_ref)

    @pl.when(step >= native)
    def _():
        add(w2_ref)

    @pl.when(step == pl.num_programs(0) - 1)
    def _():
        lane = iota((rows, 128), 1)
        packed = jnp.where(
            lane == 0, max_ref[...], jnp.where(lane == 1, sum_ref[...], jnp.where(lane == 2, hit_ref[...], 0.0))
        )
        stat_ref[...] = jnp.transpose(packed)[0:8]
        pl.semaphore_wait(barrier, peers - 1 + count - 1)
        combine_scores(
            stat_ref, valid_ref, len_ref, owner_ref, sums_ref, delta_ref,
            all_ref, part_ref, parts_ref, s_send, s_recv, p_send, p_recv,
        )


def combine_scores(
    stat_ref, valid_ref, len_ref, owner_ref, sums_ref, delta_ref,
    all_ref, part_ref, parts_ref, s_send, s_recv, p_send, p_recv,
):
    seq, mp = lax.axis_index("seq"), lax.axis_index("mp")
    peers, count = X * CORES, Y * Z
    tok = valid_ref.shape[1]

    def stats(d):
        return pltpu.make_async_remote_copy(
            src_ref=stat_ref, dst_ref=all_ref.at[mp], send_sem=s_send.at[d], recv_sem=s_recv.at[d],
            device_id=(seq, lax.rem(mp + d, peers)), device_id_type=MESH,
        )

    for d in range(1, peers):
        stats(d).start()
    all_ref[mp] = stat_ref[...]
    starts_row, roll_col, _, _ = rollout_tables(len_ref[...].astype(jnp.float32), seq * tok, tok)
    lanes = starts_row.shape[1]
    member = (roll_col == iota((tok, lanes), 1).astype(jnp.float32)).astype(jnp.float32)
    for d in range(1, peers):
        stats(d).wait_recv()
    tops = [all_ref[k][0:1] for k in range(peers)]
    top = functools.reduce(jnp.maximum, tops)
    total = functools.reduce(
        jnp.add, [all_ref[k][1:2] * jnp.exp(tops[k] - top) for k in range(peers)]
    )
    hit = functools.reduce(jnp.add, [all_ref[k][2:3] for k in range(peers)])
    logprob = hit - top - jnp.log(total)
    delta = (logprob[:, :tok] - logprob[:, tok:]) * valid_ref[...].astype(jnp.float32)
    delta_ref[...] = delta
    part_ref[...] = jnp.dot(
        jnp.broadcast_to(delta, (8, tok)), member, precision=HIGHEST, preferred_element_type=jnp.float32
    )

    def parts(d):
        return pltpu.make_async_remote_copy(
            src_ref=part_ref, dst_ref=parts_ref.at[seq], send_sem=p_send.at[d], recv_sem=p_recv.at[d],
            device_id=(lax.rem(seq + d, count), mp), device_id_type=MESH,
        )

    def begin(d, carry):
        parts(d).start()
        return carry

    def end(d, carry):
        parts(d).wait_recv()
        return carry

    def drain(d, carry):
        parts(d).wait_send()
        return carry

    lax.fori_loop(1, count, begin, 0)
    parts_ref[seq] = part_ref[...]
    lax.fori_loop(1, count, end, 0)
    sums = functools.reduce(jnp.add, [parts_ref[k] for k in range(count)])[0:1] / len_ref[...].astype(jnp.float32)
    mine = jnp.where(owner_ref[...] == seq, sums, 0.0)
    sums_ref[...] = mine[:, : sums_ref.shape[1]]
    for d in range(1, peers):
        stats(d).wait_send()
    lax.fori_loop(1, count, drain, 0)


def scores(normed, w1, w2, vocab, target, valid_row, len_row, owner_row, rolls):
    peers, count = X * CORES, Y * Z
    rows, depth = normed.shape
    tok = valid_row.shape[1]
    lanes = len_row.shape[1]
    native = w1.shape[1] // TILE
    dma = pltpu.SemaphoreType.DMA
    f32 = jnp.float32

    def fixed(shape):
        return pl.BlockSpec(shape, lambda j: (0, 0), pipeline_mode=pl.Buffered(1))

    return pl.pallas_call(
        functools.partial(scores_kernel, vocab, native),
        grid=(native + w2.shape[1] // TILE,),
        out_shape=(jax.ShapeDtypeStruct((1, rolls), f32), jax.ShapeDtypeStruct((1, tok), f32)),
        in_specs=[
            fixed((rows, depth)),
            pl.BlockSpec((depth, TILE), lambda j: (0, jnp.minimum(j, native - 1))),
            pl.BlockSpec((depth, TILE), lambda j: (0, jnp.maximum(j - native, 0))),
            fixed((rows, 1)), fixed((1, tok)), fixed((1, lanes)), fixed((1, lanes)),
        ],
        out_specs=(pl.BlockSpec((1, rolls), lambda j: (0, 0)), pl.BlockSpec((1, tok), lambda j: (0, 0))),
        scratch_shapes=[pltpu.VMEM((rows, 1), f32)] * 3
        + [
            pltpu.VMEM((8, rows), f32),
            pltpu.VMEM((peers, 8, rows), f32),
            pltpu.VMEM((8, lanes), f32),
            pltpu.VMEM((count, 8, lanes), f32),
            dma((peers,)), dma((peers,)), dma((count,)), dma((count,)),
        ],
        compiler_params=pltpu.CompilerParams(
            collective_id=3, has_side_effects=True, vmem_limit_bytes=VMEM_BYTES
        ),
        cost_estimate=pl.CostEstimate(flops=8 * 10**9, bytes_accessed=2 * 10**7, transcendentals=10**6),
        name="scores",
    )(normed, w1, w2, target, valid_row, len_row, owner_row)


def shards(
    scored_token_targets, valid, lengths, owners, holders, mixer_input_x, mixer_gate_input,
    input_projection_b, output_projection_c, token_step_sizes, head_decay_rate, head_skip_scale,
    prompt_held_states, shared_output_weight, adapter_down_weight, adapter_up_weight,
    residual, final_norm_scale, vocab_head_weight,
):
    tok = scored_token_targets.shape[0]
    models, _, inner = mixer_input_x.shape
    state = input_projection_b.shape[2]
    rolls = lengths.shape[0]
    share = tok // (X * CORES)
    mp = lax.axis_index("mp")
    vocab = vocab_head_weight.shape[1]
    head_native = lax.all_gather(vocab_head_weight[:, :HEAD_NATIVE], "seq", axis=0, tiled=True)
    rest = vocab - HEAD_NATIVE
    head_rest = jnp.pad(vocab_head_weight[:, HEAD_NATIVE:], ((0, 0), (0, -rest % TILE)))

    def row(values, fill):
        return jnp.pad(values, (0, 128 - rolls), constant_values=fill)[None, :]

    len_row, owner_row = row(lengths, 0), row(owners, -1)
    prompts = jnp.transpose(prompt_held_states[:, 0], (1, 2, 0, 3)).reshape(inner, models * state)
    own_res = jnp.transpose(lax.dynamic_slice_in_dim(residual, mp * share, share, 0), (1, 0, 2))
    x, b, c, z = (
        jnp.swapaxes(a, 1, 2)
        for a in (mixer_input_x, input_projection_b, output_projection_c, mixer_gate_input)
    )
    y, run, ends, last = local_mix(
        len_row, x, b, c, jnp.transpose(token_step_sizes, (2, 0, 1)), head_decay_rate, head_skip_scale
    )
    pall, en, dn, wos, dws = states(prompts, ends, last, shared_output_weight, adapter_down_weight)
    gated = finish_mix(
        len_row, lengths[None, :], holders[None, :], y, run, c, z,
        pall.reshape((Z * Y,) + prompts.shape), en, dn,
    )
    normed, head_own = project(
        gated, shared_output_weight, wos, adapter_down_weight, dws, adapter_up_weight, own_res,
        final_norm_scale[None, :], head_rest,
    )
    local = scored_token_targets - mp * vocab
    target = jnp.concatenate([local, local])[:, None]
    sums, delta = scores(
        normed.reshape(models * tok, -1), head_native, head_own.reshape(-1, head_rest.shape[1]), vocab,
        target, valid[None, :], len_row, owner_row, rolls,
    )
    return sums, delta.reshape(tok)


def solution(mesh):
    placed = (
        P("seq"), P("seq"), P(), P(), P(),
        P(None, "seq", "mp"), P(None, "seq", "mp"),
        P(None, "seq", None), P(None, "seq", None), P(None, "seq", "mp"),
        P(None, "mp"), P(None, "mp"), P(None, "seq", "mp", None, None),
        P("mp", None), P("mp", None), P(), P("seq", None, None), P(), P("seq", "mp"),
    )
    return jax.shard_map(
        shards, mesh=mesh, in_specs=placed, out_specs=(P("seq", None), P("seq")), check_vma=False
    )
```

time: 237 us -> 203 us (0.86)
  Pallas kernels: 202 us -> 176 us
  local copies, waits for them, and re-layouts: 17.6 us -> 11 us
    pallas_call x1, Pallas kernels: 94.9 us -> 55.7 us  [states(): pl.pallas_call(states_kernel, out_shape=out, in_specs=[anywhere()] * 5, o...]
    pallas_call x3 -> x2, Pallas kernels: 92.9 us -> 111 us  [the longest x1 75.4 us: project(): pl.pallas_call(project_kernel, out_shape=(jax.ShapeDtypeStruct((models, X...]
    unnamed x18 -> x11, local copies, waits for them, and re-layouts: 12 us -> 3.3 us
    pallas_call x1, Pallas kernels: 7.46 us -> 4.48 us  [local_mix(): pl.pallas_call(local_mix_kernel, out_shape=(jax.ShapeDtypeStruct((models,...]
  transfers between devices with their start and end apart: 1 -> 1, of which waited for: 0 -> 0; matrix products, arithmetic and copies ran while one was open for 6% -> 3% of each run, Pallas kernels for 70% -> 70%
where the time goes in v2:
time: 203 us; the launch traced here: 201 us
  Pallas kernels  176 us (87%)
  between operations  14.1 us (7%)
  local copies, waits for them, and re-layouts  11 us (5%)
    pallas_call x1, Pallas kernels, project(): pl.pallas_call(project_kernel, out_shape=(jax.ShapeDtypeStruct((models, X...  75.4 us
    pallas_call x1, Pallas kernels, states(): pl.pallas_call(states_kernel, out_shape=out, in_specs=[anywhere()] * 5, o...  55.7 us
    pallas_call x1, Pallas kernels, scores(): pl.pallas_call(functools.partial(scores_kernel, vocab, native), grid=(nat...  35.3 us
    pallas_call x1, Pallas kernels, finish_mix(): pl.pallas_call(finish_mix_kernel, out_shape=jax.ShapeDtypeStruct((models,...  5.22 us
    pallas_call x1, Pallas kernels, local_mix(): pl.pallas_call(local_mix_kernel, out_shape=(jax.ShapeDtypeStruct((models,...  4.48 us
  transfers between devices with their start and end apart: 1, of which 0 were waited for; matrix products, arithmetic and copies ran while one was open for 3% of the time, Pallas kernels for 70%

profile of v2, /device:TPU:0, one launch (start us, length us, event | category | flops | bytes accessed | tf_op | source)
XLA Modules:
  0.0 201.3 jit_solution(18413271450360286123)
XLA Ops:
  7.2 0.0 slice-start
  7.2 0.0 copy-start
  7.2 0.0 copy-start.2
  7.2 0.0 copy-start.1
  7.2 0.0 copy-start.3
  7.2 0.0 all-gather.2.cloned.1.call-start
  7.3 1.7 slice.7
  9.0 0.0 all-gather.2.cloned.1.call-update
  9.0 1.2 copy.23
  10.2 0.8 reshape.22.pt_ref
  11.0 1.3 constant_dynamic-slice_fusion
  12.3 0.9 copy.28
  13.2 0.0 copy-done
  13.2 0.6 broadcast_in_dim.24.scale_ref
  13.8 0.0 copy-done.2
  13.8 0.9 copy.25.tgt_ref
  14.7 0.0 slice-done
  14.7 0.7 pad.12.head_ref
  15.4 0.0 copy-done.1
  15.4 0.0 copy-done.3
  15.4 0.5 pad_bitcast_fusion
  15.9 4.5 %local_mix.1 = (f32[2,448,256]{2,1,0:T(8,128)}, f32[2,8,256]{2,1,0:T(8,128)}, bf16[448,128]{1,0:T(8,128)(2,1)}, f32[8,128]{1,0:T(8,128)}) custom-call(s32[1,128]{1,0:T(1,128)} %get-tuple-element.29.len_ref, bf16[2,448,256]{2,1,0:T(8,128)(2,1)} %bitcast.35, bf16[2,64,256]{2,1,0:T(8,128)(2,1)} %bitcast.36, bf16[2,64,256]{2,1,0:T(8,128)(2,1)} %bitcast.29, ...), custom_call_target="tpu_custom_call" | custom-call | flops 2000000000 | bytes 4000000 | tf_op jit(solution)/shard_map/local_mix/pallas_call | solution.py:99
  20.4 55.7 %state_exchange.1 = (bf16[8,4,448,128]{3,2,1,0:T(8,128)(2,1)}, bf16[4,448,128]{2,1,0:T(8,128)(2,1)}, f32[4,8,128]{2,1,0:T(8,128)}, bf16[448,3584]{1,0:T(8,128)(2,1)}, bf16[448,128]{1,0:T(8,128)(2,1)}) custom-call(bf16[448,128]{1,0:T(8,128)(2,1)} %reshape.22.pt_ref, bf16[448,128]{1,0:T(8,128)(2,1)} %get-tuple-element.17.e_ref, ...), custom_call_target="tpu_custom_call" | custom-call | bytes 100000000 | tf_op jit(solution)/shard_map/state_exchange/pallas_call | solution.py:285
  76.1 5.2 %finish_mix.1 = bf16[2,256,448]{2,1,0:T(8,128)(2,1)} custom-call(s32[1,48]{1,0:T(1,128)} %bitcast.32, s32[1,48]{1,0:T(1,128)} %bitcast.34, s32[1,128]{1,0:T(1,128)} %get-tuple-element.29.len_ref, f32[2,448,256]{2,1,0:T(8,128)} %get-tuple-element.15.y_ref, f32[2,8,256]{2,1,0:T(8,128)} %get-tuple-element.16.run_ref, bf16[2,64,256]{2,1,0:T(8,128)(2,1)} %bitcast.30, ...), custom_call_target="tpu_custom_call" | custom-call | flops 1000000000 | bytes 8000000 | tf_op jit(solution)/shard_map/finish_mix/pallas_call | solution.py:380
  81.3 75.4 %project_norm.1 = (bf16[2,8,32,3584]{3,2,1,0:T(8,128)(2,1)}, bf16[8,4,112,1024]{3,2,1,0:T(8,128)(2,1)}) custom-call(bf16[2,4,2,32,448]{4,3,2,1,0:T(8,128)(2,1)} %bitcast.25, bf16[448,3584]{1,0:T(8,128)(2,1)} %wo_ref.3, bf16[448,3584]{1,0:T(8,128)(2,1)} %get-tuple-element.22.wos_ref, bf16[448,128]{1,0:T(8,128)(2,1)} %dw_ref.3, ...), custom_call_target="tpu_custom_call" | custom-call | flops 10000000000 | bytes 100000000 | tf_op jit(solution)/shard_map/project_norm/pallas_call | solution.py:533
  156.7 0.0 all-gather.2.cloned.1.call-done.w1_ref
  156.7 35.3 %scores.1 = (f32[1,48]{1,0:T(1,128)}, f32[1,256]{1,0:T(1,128)}) custom-call(bf16[512,3584]{1,0:T(8,128)(2,1)} %bitcast.40, bf16[3584,1024]{1,0:T(8,128)(2,1)} %all-gather.2.cloned.1.call-done.w1_ref, bf16[3584,1024]{1,0:T(8,128)(2,1)} %bitcast.39, s32[512,1]{1,0:T(8,128)} %copy.25.tgt_ref, s32[1,256]{1,0:T(1,128)} %bitcast.38, ...), custom_call_target="tpu_custom_call" | custom-call | flops 8000000000 | bytes 20000000 | tf_op jit(solution)/shard_map/scores/pallas_call | solution.py:694
  192.0 1.2 copy.31
  193.2 1.2 copy.32
  (2 shorter events, 0.0 us)
Async XLA Ops:
  7.2 7.5 %slice-start = ((bf16[112,2000]{1,0:T(8,128)(2,1)}), bf16[112,976]{1,0:T(8,128)(2,1)S(1)}, s32[]{:S(2)}) async-start(bf16[112,2000]{1,0:T(8,128)(2,1)} %param.37), calls=%async_computation.1 | async-start | bytes 458752 | tf_op jit(solution)/shard_map/slice | solution.py:736
  7.2 6.0 %copy-start = (f32[3584]{0:T(1024)S(1)}, f32[3584]{0:T(1024)}, u32[]{:S(2)}) copy-start(f32[3584]{0:T(1024)} %param.36) | copy-start | bytes 43012
  7.2 6.6 %copy-start.2 = (s32[256]{0:T(256)S(1)}, s32[256]{0:T(256)}, u32[]{:S(2)}) copy-start(s32[256]{0:T(256)} %param.19) | copy-start | bytes 3076
  7.2 8.2 %copy-start.1 = (s32[48]{0:T(128)S(1)}, s32[48]{0:T(128)}, u32[]{:S(2)}) copy-start(s32[48]{0:T(128)} %param.21) | copy-start | bytes 580
  7.2 8.2 %copy-start.3 = (s32[48]{0:T(128)S(1)}, s32[48]{0:T(128)}, u32[]{:S(2)}) copy-start(s32[48]{0:T(128)} %param.22) | copy-start | bytes 580
  7.2 149.5 %all-gather.2.cloned.1.call-start = ((), (), s32[]{:S(2)}) async-start(), calls=%async_computation | async-start | bytes 7569408 | tf_op jit(solution)/shard_map/all_gather | solution.py:734
Sparse Core Ops, SparseCore 0:
  10.6 113.1 all-gather.1

commit v3 on v2

--- a/solution.py
+++ b/solution.py
@@ -233,11 +233,11 @@
 
 
 def states_kernel(
-    pt_ref, e_ref, dl_ref, wo_ref, dw_ref,
-    pall_ref, en_ref, dn_ref, wos_ref, dws_ref,
+    pt_ref, e_ref, dl_ref, wo_ref, dw_ref, tgt_ref,
+    pall_ref, en_ref, dn_ref, wos_ref, dws_ref, tgp_ref,
     send_sem, recv_sem, own_sem,
 ):
-    seq, mp, _, _, at_y, at_z = place()
+    seq, mp, _, y, at_y, at_z = place()
     count = Y * Z
 
     def at_s(d):
@@ -259,6 +259,7 @@
         waits.append(send(dl_ref, dn_ref.at[d - 1], at_s(d)))
     waits.append(send(wo_ref, wos_ref, sibling))
     waits.append(send(dw_ref, dws_ref, sibling))
+    waits.append(send(tgt_ref, tgp_ref, partner_of(at_y, y)))
     for _ in ring:
         pass
     for copy in waits:
@@ -268,25 +269,25 @@
 
 
 PROMPT_SPLIT = 192
-HEAD_SPLIT = 48
-HEAD_NATIVE = 1024
+PAIR_SPLIT = 64
 TILE = 256
 
 
-def states(pt, e, dl, wo, dw):
+def states(pt, e, dl, wo, dw, tgt):
     out = (
         jax.ShapeDtypeStruct((Z, Y) + pt.shape, pt.dtype),
         jax.ShapeDtypeStruct((REACH,) + e.shape, e.dtype),
         jax.ShapeDtypeStruct((REACH,) + dl.shape, dl.dtype),
         jax.ShapeDtypeStruct(wo.shape, wo.dtype),
         jax.ShapeDtypeStruct(dw.shape, dw.dtype),
-    )
-    copies = RING_COPIES + 2 * REACH + 2
+        jax.ShapeDtypeStruct(tgt.shape, tgt.dtype),
+    )
+    copies = RING_COPIES + 2 * REACH + 3
     return pl.pallas_call(
         states_kernel,
         out_shape=out,
-        in_specs=[anywhere()] * 5,
-        out_specs=(anywhere(),) * 5,
+        in_specs=[anywhere()] * 6,
+        out_specs=(anywhere(),) * 6,
         scratch_shapes=[
             pltpu.SemaphoreType.DMA((copies,)),
             pltpu.SemaphoreType.DMA((copies,)),
@@ -297,7 +298,7 @@
         ),
         cost_estimate=pl.CostEstimate(flops=0, bytes_accessed=10**8, transcendentals=0),
         name="state_exchange",
-    )(pt, e, dl, wo, dw)
+    )(pt, e, dl, wo, dw, tgt)
 
 
 def finish_mix_kernel(
@@ -389,13 +390,124 @@
     )(lengths, holders, len_row, y, run, c, z, pall, en, dn)
 
 
-def project_kernel(
-    g_ref, wo_ref, wos_ref, dw_ref, dws_ref, up_ref, res_ref, scale_ref, head_ref, nall_ref, wall_ref,
-    gs_ref, low_ref, acc_ref, out_ref, comb_ref, relay_ref, direct_ref, sum_ref, h_ref, n_ref,
-    send_sem, recv_sem, ring_send, ring_recv, own_sem, keep_sem,
+def pair_ring(send, w_ref, wall_ref, oth_ref, split, own_sem):
+    _, _, z, y, at_y, at_z = place()
+    toward = 1 - 2 * lax.rem(y, 2)
+    same, other = at_y(toward), at_y(-toward)
+    y_other = lax.rem(y - toward + Y, Y)
+    mine = y // 2
+    rows = w_ref.shape[1]
+    count = rows - split
+    half = count // 32 * 16
+    first, second = pl.ds(0, split), pl.ds(split, count)
+    low, high = pl.ds(split, half), pl.ds(split + half, count - half)
+    low_o, high_o = pl.ds(0, half), pl.ds(half, count - half)
+
+    def zz(d):
+        return lax.rem(z + d + Z, Z)
+
+    def along(ref, peer):
+        return send(ref, ref, peer)
+
+    pending, last = [], []
+
+    def to_y(d):
+        j = zz(d)
+        dst = wall_ref.at[j, y, second]
+        src_same = dst if d else w_ref.at[mine, second]
+        src_other = oth_ref.at[j] if d else w_ref.at[1 - mine, second]
+        pending.append((j, send(src_same, dst, same), send(src_other, dst, other)))
+
+    def pass_y():
+        j, from_same, from_other = pending.pop(0)
+        from_other.wait_recv()
+        last.append(along(wall_ref.at[j, y_other, second], same))
+        last.append(from_same)
+
+    def along_z(d, rows_w, rows_o, peer):
+        return [along(wall_ref.at[zz(d), y, rows_w], peer), along(oth_ref.at[zz(d), rows_o], peer)]
+
+    keep = pltpu.make_async_copy(w_ref.at[mine], wall_ref.at[z, y], own_sem)
+    keep.start()
+    a_same = send(w_ref.at[mine, first], wall_ref.at[z, y, first], same)
+    a_other = send(w_ref.at[1 - mine, first], wall_ref.at[z, y, first], other)
+    right, left = (
+        [
+            send(w_ref.at[mine, second], wall_ref.at[z, y, second], at_z(d)),
+            send(w_ref.at[1 - mine, second], oth_ref.at[z], at_z(d)),
+        ]
+        for d in (1, -1)
+    )
+    to_y(0)
+    keep.wait()
+    yield
+    a_other.wait_recv()
+    a_pass = along(wall_ref.at[z, y_other, first], same)
+    a_same.wait_recv()
+    yield
+    a_pass.wait_recv()
+    group = wall_ref.at[z, :, first]
+    far_right, far_left = along(group, at_z(1)), along(group, at_z(-1))
+    yield
+    everything = pl.ds(0, count)
+    for k in range(1, Z // 2):
+        whole = k < Z // 2 - 1
+        for copy in right:
+            copy.wait_recv()
+        right = along_z(-k, second if whole else low, everything if whole else low_o, at_z(1))
+        to_y(-k)
+        for copy in left:
+            copy.wait_recv()
+        left = along_z(k, second if whole else high, everything if whole else high_o, at_z(-1))
+        to_y(k)
+        yield
+        pass_y()
+        yield
+        if k > 1:
+            far_right.wait_recv()
+            far_right = along(wall_ref.at[zz(1 - k), :, first], at_z(1))
+            far_left.wait_recv()
+            far_left = along(wall_ref.at[zz(k - 1), :, first], at_z(-1))
+            yield
+    for copy in right + left:
+        copy.wait_recv()
+    to_y(Z // 2)
+    yield
+    pass_y()
+    pass_y()
+    yield
+    far_right.wait_recv()
+    far_right = along(wall_ref.at[zz(1 - Z // 2), pl.ds(0, Y // 2), first], at_z(1))
+    far_left.wait_recv()
+    far_left = along(wall_ref.at[zz(Z // 2 - 1), pl.ds(Y // 2, Y // 2), first], at_z(-1))
+    yield
+    while pending:
+        pass_y()
+        yield
+    far_right.wait_recv()
+    far_left.wait_recv()
+    for copy in last:
+        copy.wait_recv()
+
+
+PAIR_COPIES = 3 + 8 + 4 + 12 + 16 + 8
+
+
+def partner_of(at_y, y):
+    return at_y(2 * lax.rem(y, 2) - 1)
+
+
+def finale_kernel(
+    vocab,
+    g_ref, wo_ref, wos_ref, dw_ref, dws_ref, up_ref, res_ref, scale_ref, head_ref,
+    tgt_ref, tgp_ref, valid_ref, len_ref, owner_ref, sums_ref, delta_ref,
+    gs_ref, low_ref, acc_ref, out_ref, comb_ref, relay_ref, direct_ref, sum_ref, h_ref, nall_ref, wall_ref, oth_ref,
+    max_ref, exp_ref, hit_ref, want_ref, stat_ref, all_ref, part_ref, parts_ref,
+    send_sem, recv_sem, ring_send, ring_recv, own_sem, s_send, s_recv, p_send, p_recv,
 ):
-    seq, mp, _, _, at_y, at_z = place()
+    seq, mp, z, y, at_y, at_z = place()
     x, core = mp // CORES, lax.rem(mp, CORES)
+    peers, count = X * CORES, Y * Z
     chunks = acc_ref.shape[0]
     width = acc_ref.shape[4]
     share = res_ref.shape[1]
@@ -403,6 +515,7 @@
     inner = g_ref.shape[4]
     rows = X * share
     sibling = (seq, x * CORES + 1 - core)
+    partner = partner_of(at_y, y)
 
     def xx(d):
         return lax.rem(x + d + X, X)
@@ -410,14 +523,25 @@
     def at_x(d):
         return (seq, xx(d) * CORES + core)
 
-    greet(
-        pltpu.get_barrier_semaphore(),
-        [sibling, at_x(1), at_x(-1), at_y(1), at_y(-1), at_y(2), at_z(1), at_z(-1)],
-    )
+    barrier = pltpu.get_barrier_semaphore()
+    for d in range(1, peers):
+        pl.semaphore_signal(barrier, inc=1, device_id=(seq, lax.rem(mp + d, peers)), device_id_type=MESH)
+    for d in range(peers):
+        pl.semaphore_signal(
+            barrier, inc=1, device_id=(partner[0], lax.rem(mp + d, peers)), device_id_type=MESH
+        )
+
+    def hello(d, carry):
+        pl.semaphore_signal(barrier, inc=1, device_id=(lax.rem(seq + d, count), mp), device_id_type=MESH)
+        return carry
+
+    lax.fori_loop(1, count, hello, 0)
+    pl.semaphore_wait(barrier, 2 * peers - 1 + count - 1)
+
     send, begun = make_sender(send_sem, recv_sem)
     ring_out, ring_begun = make_sender(ring_send, ring_recv)
     gated = send(g_ref.at[:, :, 1 - core], gs_ref, sibling)
-    ring = torus_ring(ring_out, head_ref, wall_ref, HEAD_SPLIT, own_sem)
+    ring = pair_ring(ring_out, head_ref, wall_ref, oth_ref, PAIR_SPLIT, own_sem)
 
     def ring_step(times=1):
         for _ in range(times):
@@ -486,41 +610,159 @@
         square = square + jnp.stack(squares)
         if n in (1, 3, 5):
             ring_step()
-    n_ref[...] = (h_ref[...] * lax.rsqrt(square / model_width + 1e-05) * scale_ref[...]).astype(jnp.bfloat16)
-
-    def block(d, m):
-        return nall_ref.at[m, xx(d) * CORES + core]
-
-    near = [[None, None], [None, None]]
-    for side, d, m in ((0, 1, 0), (1, -1, 1), (0, 1, 1), (1, -1, 0)):
-        near[side][m] = send(n_ref.at[m], block(0, m), at_x(d))
-    shared = [send(n_ref.at[m], block(0, m), sibling) for m in range(2)]
-    keep = pltpu.make_async_copy(n_ref, nall_ref.at[:, mp], keep_sem)
-    keep.start()
+    normed = (h_ref[...] * lax.rsqrt(square / model_width + 1e-05) * scale_ref[...]).astype(jnp.bfloat16)
+    for m in range(2):
+        nall_ref[0, m, mp] = normed[m]
+
+    def block(p, d, m):
+        return nall_ref.at[p, m, xx(d) * CORES + core]
+
+    near, far, shared = [{}, {}], [{}, {}], []
+
+    def near_sends(p):
+        for side, d, m in ((0, 1, 0), (1, -1, 1), (0, 1, 1), (1, -1, 0)):
+            near[p][side, m] = send(block(p, 0, m), block(p, 0, m), at_x(d))
+        for m in range(2):
+            shared.append(send(block(p, 0, m), block(p, 0, m), sibling))
+
+    def far_sends(p):
+        for side, d, m in ((0, 1, 0), (1, -1, 1)):
+            near[p][side, m].wait_recv()
+            far[p][side] = send(block(p, -d, m), block(p, -d, m), at_x(d))
+            shared.append(send(block(p, -d, m), block(p, -d, m), sibling))
+
+    def rest(p):
+        for side, d, m in ((0, 1, 1), (1, -1, 0)):
+            near[p][side, m].wait_recv()
+            shared.append(send(block(p, -d, m), block(p, -d, m), sibling))
+
+    def beyond(p):
+        for side, m in ((0, 0), (1, 1)):
+            far[p][side].wait_recv()
+            shared.append(send(block(p, 2, m), block(p, 2, m), sibling))
+
+    to_partner = [send(block(0, 0, m), nall_ref.at[1, m, mp], partner) for m in range(2)]
+    near_sends(0)
     ring_step()
-    far = []
-    for side, d, m in ((0, 1, 0), (1, -1, 1)):
-        near[side][m].wait_recv()
-        far.append(send(block(-d, m), block(-d, m), at_x(d)))
-        shared.append(send(block(-d, m), block(-d, m), sibling))
-    ring_step(2)
-    for side, d, m in ((0, 1, 1), (1, -1, 0)):
-        near[side][m].wait_recv()
-        shared.append(send(block(-d, m), block(-d, m), sibling))
-    ring_step(2)
-    for side, m in ((0, 0), (1, 1)):
-        far[side].wait_recv()
-        shared.append(send(block(2, m), block(2, m), sibling))
+    far_sends(0)
+    ring_step()
+    for copy in to_partner:
+        copy.wait_recv()
+    near_sends(1)
+    rest(0)
+    ring_step()
+    beyond(0)
+    ring_step()
+    far_sends(1)
+    ring_step()
+    rest(1)
+    ring_step()
+    beyond(1)
+    eye = (iota((rows * 2, rows * 2), 0) == iota((rows * 2, rows * 2), 1)).astype(jnp.float32)
+    for p, ref in ((0, tgt_ref), (1, tgp_ref)):
+        column = lax.dot_general(
+            eye, ref[...], (((1,), (1,)), ((), ())), precision=HIGHEST, preferred_element_type=jnp.float32
+        )[:, 0:1]
+        want_ref[p, 0 : rows * 2, :] = column
+        want_ref[p, rows * 2 : rows * 4, :] = column
+    max_ref[...] = jnp.full(max_ref.shape, -3e38, jnp.float32)
+    exp_ref[...] = jnp.zeros(exp_ref.shape, jnp.float32)
+    hit_ref[...] = jnp.zeros(hit_ref.shape, jnp.float32)
     for _ in ring:
         pass
-    keep.wait()
     for copy in shared:
         copy.wait_recv()
+
+    tiles = wall_ref.shape[3] // TILE
+    depth = wall_ref.shape[0] * wall_ref.shape[1] * wall_ref.shape[2]
+    base = (y // 2) * wall_ref.shape[3]
+    all_rows = rows * 4
+
+    def score(i, carry):
+        p, j = i // tiles, lax.rem(i, tiles)
+        cols = pl.ds(pl.multiple_of(j * TILE, TILE), TILE)
+        logits = jnp.dot(
+            nall_ref[p].reshape(all_rows, depth), wall_ref[:, :, :, cols].reshape(depth, TILE),
+            preferred_element_type=jnp.float32,
+        )
+        col = iota((all_rows, TILE), 1) + (base + j * TILE)
+        real = col < vocab
+        wanted = col.astype(jnp.float32) + jnp.float32(1) * (mp * vocab) == want_ref[p]
+        logits = jnp.where(real, logits, -3e38)
+        top = jnp.maximum(max_ref[p], jnp.max(logits, axis=1, keepdims=True))
+        exp_ref[p] = exp_ref[p] * jnp.exp(max_ref[p] - top) + jnp.sum(
+            jnp.where(real, jnp.exp(logits - top), 0.0), axis=1, keepdims=True
+        )
+        max_ref[p] = top
+        hit_ref[p] += jnp.sum(jnp.where(real & wanted, logits, 0.0), axis=1, keepdims=True)
+        return carry
+
+    lax.fori_loop(0, 2 * tiles, score, 0)
+    lane = iota((all_rows, 128), 1)
+    for p in range(2):
+        packed = jnp.where(
+            lane == 0, max_ref[p], jnp.where(lane == 1, exp_ref[p], jnp.where(lane == 2, hit_ref[p], 0.0))
+        )
+        stat_ref[p] = jnp.transpose(packed)[0:8]
+
+    def stats(p, d):
+        return pltpu.make_async_remote_copy(
+            src_ref=stat_ref.at[p], dst_ref=all_ref.at[p, mp], send_sem=s_send.at[p, d], recv_sem=s_recv.at[p, d],
+            device_id=(partner[0] if p else seq, lax.rem(mp + d, peers)), device_id_type=MESH,
+        )
+
+    exchange = [(1, d) for d in range(peers)] + [(0, d) for d in range(1, peers)]
+    for p, d in exchange:
+        stats(p, d).start()
+    all_ref[0, mp] = stat_ref[0]
+    tok = valid_ref.shape[1]
+    starts_row, roll_col, _, _ = rollout_tables(len_ref[...].astype(jnp.float32), seq * tok, tok)
+    lanes = starts_row.shape[1]
+    member = (roll_col == iota((tok, lanes), 1).astype(jnp.float32)).astype(jnp.float32)
     for copy in begun + ring_begun:
         copy.wait_send()
-
-
-def project(gated, wo, wos, dw, dws, up, res, scale, head):
+    for p, d in exchange:
+        stats(p, d).wait_recv()
+    found = [all_ref[p, k] for p in range(2) for k in range(peers)]
+    top = functools.reduce(jnp.maximum, [f[0:1] for f in found])
+    total = functools.reduce(jnp.add, [f[1:2] * jnp.exp(f[0:1] - top) for f in found])
+    hit = functools.reduce(jnp.add, [f[2:3] for f in found])
+    logprob = hit - top - jnp.log(total)
+    delta = (logprob[:, :tok] - logprob[:, tok:]) * valid_ref[...].astype(jnp.float32)
+    delta_ref[...] = delta
+    part_ref[...] = jnp.dot(
+        jnp.broadcast_to(delta, (8, tok)), member, precision=HIGHEST, preferred_element_type=jnp.float32
+    )
+
+    def parts(d):
+        return pltpu.make_async_remote_copy(
+            src_ref=part_ref, dst_ref=parts_ref.at[seq], send_sem=p_send.at[d], recv_sem=p_recv.at[d],
+            device_id=(lax.rem(seq + d, count), mp), device_id_type=MESH,
+        )
+
+    def begin(d, carry):
+        parts(d).start()
+        return carry
+
+    def end(d, carry):
+        parts(d).wait_recv()
+        return carry
+
+    def drain(d, carry):
+        parts(d).wait_send()
+        return carry
+
+    lax.fori_loop(1, count, begin, 0)
+    parts_ref[seq] = part_ref[...]
+    for p, d in exchange:
+        stats(p, d).wait_send()
+    lax.fori_loop(1, count, end, 0)
+    means = functools.reduce(jnp.add, [parts_ref[k] for k in range(count)])[0:1] / len_ref[...].astype(jnp.float32)
+    sums_ref[...] = jnp.where(owner_ref[...] == seq, means, 0.0)[:, : sums_ref.shape[1]]
+    lax.fori_loop(1, count, drain, 0)
+
+
+def finale(vocab, gated, wo, wos, dw, dws, up, res, scale, head, tgt, tgp, valid_row, len_row, owner_row, rolls):
     models, tok, inner = gated.shape
     width_all = wo.shape[1]
     share = res.shape[1]
@@ -528,16 +770,17 @@
     chunks = width_all // width
     bf16, f32 = jnp.bfloat16, jnp.float32
     dma = pltpu.SemaphoreType.DMA
-    copies = 1 + 6 * chunks + 4 + 2 + 2 + 6
+    copies = 1 + 6 * chunks + 2 + 2 * 14
+    peers, count = X * CORES, Y * Z
     piece = pltpu.VMEM((chunks, 2, share, width), bf16)
+    column = pltpu.VMEM((2, models * tok, 1), f32)
+    _, head_rows, head_cols = head.shape
+    lanes = len_row.shape[1]
     return pl.pallas_call(
-        project_kernel,
-        out_shape=(
-            jax.ShapeDtypeStruct((models, X * CORES, share, width_all), bf16),
-            jax.ShapeDtypeStruct((Z, Y) + head.shape, bf16),
-        ),
-        in_specs=[vmem()] * 8 + [anywhere()],
-        out_specs=(anywhere(),) * 2,
+        functools.partial(finale_kernel, vocab),
+        out_shape=(jax.ShapeDtypeStruct((1, rolls), f32), jax.ShapeDtypeStruct((1, tok), f32)),
+        in_specs=[vmem()] * 8 + [anywhere()] + [vmem()] * 5,
+        out_specs=(vmem(),) * 2,
         scratch_shapes=[
             pltpu.VMEM((models, X, share, inner), bf16),
             pltpu.VMEM((X * share, dw.shape[1]), bf16),
@@ -545,177 +788,26 @@
             pltpu.VMEM((chunks, models, X, share, width), bf16),
             piece, piece, piece, piece,
             pltpu.VMEM((models, share, width_all), f32),
-            pltpu.VMEM((models, share, width_all), bf16),
-            dma((copies,)), dma((copies,)), dma((RING_COPIES,)), dma((RING_COPIES,)), dma, dma,
+            pltpu.VMEM((2, models, peers, share, width_all), bf16),
+            pltpu.VMEM((Z, Y, head_rows, head_cols), bf16),
+            pltpu.VMEM((Z, head_rows - PAIR_SPLIT, head_cols), bf16),
+            column, column, column, column,
+            pltpu.VMEM((2, 8, models * tok), f32),
+            pltpu.VMEM((2, peers, 8, models * tok), f32),
+            pltpu.VMEM((8, lanes), f32),
+            pltpu.VMEM((count, 8, lanes), f32),
+            dma((copies,)), dma((copies,)), dma((PAIR_COPIES,)), dma((PAIR_COPIES,)), dma,
+            dma((2, peers)), dma((2, peers)), dma((count,)), dma((count,)),
         ],
         compiler_params=pltpu.CompilerParams(
             collective_id=2, has_side_effects=True, vmem_limit_bytes=VMEM_BYTES
         ),
-        cost_estimate=pl.CostEstimate(flops=10**10, bytes_accessed=10**8, transcendentals=0),
-        name="project_norm",
-    )(gated.reshape(models, X, CORES, share, inner), wo, wos, dw, dws, up, res, scale, head)
-
-
-def scores_kernel(
-    vocab, native, n_ref, w1_ref, w2_ref, tgt_ref, valid_ref, len_ref, owner_ref, sums_ref, delta_ref,
-    max_ref, sum_ref, hit_ref, stat_ref, all_ref, part_ref, parts_ref, s_send, s_recv, p_send, p_recv,
-):
-    seq, mp = lax.axis_index("seq"), lax.axis_index("mp")
-    peers, count = X * CORES, Y * Z
-    step = pl.program_id(0)
-    tile = w1_ref.shape[1]
-    rows = n_ref.shape[0]
-    barrier = pltpu.get_barrier_semaphore()
-
-    @pl.when(step == 0)
-    def _():
-        for d in range(1, peers):
-            pl.semaphore_signal(barrier, inc=1, device_id=(seq, lax.rem(mp + d, peers)), device_id_type=MESH)
-
-        def hello(d, carry):
-            pl.semaphore_signal(barrier, inc=1, device_id=(lax.rem(seq + d, count), mp), device_id_type=MESH)
-            return carry
-
-        lax.fori_loop(1, count, hello, 0)
-        max_ref[...] = jnp.full(max_ref.shape, -3e38, jnp.float32)
-        sum_ref[...] = jnp.zeros(sum_ref.shape, jnp.float32)
-        hit_ref[...] = jnp.zeros(hit_ref.shape, jnp.float32)
-
-    def add(w_ref):
-        logits = jnp.dot(n_ref[...], w_ref[...], preferred_element_type=jnp.float32)
-        col = iota((rows, tile), 1) + step * tile
-        real = col < vocab
-        logits = jnp.where(real, logits, -3e38)
-        top = jnp.maximum(max_ref[...], jnp.max(logits, axis=1, keepdims=True))
-        sum_ref[...] = sum_ref[...] * jnp.exp(max_ref[...] - top) + jnp.sum(
-            jnp.where(real, jnp.exp(logits - top), 0.0), axis=1, keepdims=True
-        )
-        max_ref[...] = top
-        hit_ref[...] += jnp.sum(jnp.where(real & (col == tgt_ref[...]), logits, 0.0), axis=1, keepdims=True)
-
-    @pl.when(step < native)
-    def _():
-        add(w1_ref)
-
-    @pl.when(step >= native)
-    def _():
-        add(w2_ref)
-
-    @pl.when(step == pl.num_programs(0) - 1)
-    def _():
-        lane = iota((rows, 128), 1)
-        packed = jnp.where(
-            lane == 0, max_ref[...], jnp.where(lane == 1, sum_ref[...], jnp.where(lane == 2, hit_ref[...], 0.0))
-        )
-        stat_ref[...] = jnp.transpose(packed)[0:8]
-        pl.semaphore_wait(barrier, peers - 1 + count - 1)
-        combine_scores(
-            stat_ref, valid_ref, len_ref, owner_ref, sums_ref, delta_ref,
-            all_ref, part_ref, parts_ref, s_send, s_recv, p_send, p_recv,
-        )
-
-
-def combine_scores(
-    stat_ref, valid_ref, len_ref, owner_ref, sums_ref, delta_ref,
-    all_ref, part_ref, parts_ref, s_send, s_recv, p_send, p_recv,
-):
-    seq, mp = lax.axis_index("seq"), lax.axis_index("mp")
-    peers, count = X * CORES, Y * Z
-    tok = valid_ref.shape[1]
-
-    def stats(d):
-        return pltpu.make_async_remote_copy(
-            src_ref=stat_ref, dst_ref=all_ref.at[mp], send_sem=s_send.at[d], recv_sem=s_recv.at[d],
-            device_id=(seq, lax.rem(mp + d, peers)), device_id_type=MESH,
-        )
-
-    for d in range(1, peers):
-        stats(d).start()
-    all_ref[mp] = stat_ref[...]
-    starts_row, roll_col, _, _ = rollout_tables(len_ref[...].astype(jnp.float32), seq * tok, tok)
-    lanes = starts_row.shape[1]
-    member = (roll_col == iota((tok, lanes), 1).astype(jnp.float32)).astype(jnp.float32)
-    for d in range(1, peers):
-        stats(d).wait_recv()
-    tops = [all_ref[k][0:1] for k in range(peers)]
-    top = functools.reduce(jnp.maximum, tops)
-    total = functools.reduce(
-        jnp.add, [all_ref[k][1:2] * jnp.exp(tops[k] - top) for k in range(peers)]
-    )
-    hit = functools.reduce(jnp.add, [all_ref[k][2:3] for k in range(peers)])
-    logprob = hit - top - jnp.log(total)
-    delta = (logprob[:, :tok] - logprob[:, tok:]) * valid_ref[...].astype(jnp.float32)
-    delta_ref[...] = delta
-    part_ref[...] = jnp.dot(
-        jnp.broadcast_to(delta, (8, tok)), member, precision=HIGHEST, preferred_element_type=jnp.float32
-    )
-
-    def parts(d):
-        return pltpu.make_async_remote_copy(
-            src_ref=part_ref, dst_ref=parts_ref.at[seq], send_sem=p_send.at[d], recv_sem=p_recv.at[d],
-            device_id=(lax.rem(seq + d, count), mp), device_id_type=MESH,
-        )
-
-    def begin(d, carry):
-        parts(d).start()
-        return carry
-
-    def end(d, carry):
-        parts(d).wait_recv()
-        return carry
-
-    def drain(d, carry):
-        parts(d).wait_send()
-        return carry
-
-    lax.fori_loop(1, count, begin, 0)
-    parts_ref[seq] = part_ref[...]
-    lax.fori_loop(1, count, end, 0)
-    sums = functools.reduce(jnp.add, [parts_ref[k] for k in range(count)])[0:1] / len_ref[...].astype(jnp.float32)
-    mine = jnp.where(owner_ref[...] == seq, sums, 0.0)
-    sums_ref[...] = mine[:, : sums_ref.shape[1]]
-    for d in range(1, peers):
-        stats(d).wait_send()
-    lax.fori_loop(1, count, drain, 0)
-
-
-def scores(normed, w1, w2, vocab, target, valid_row, len_row, owner_row, rolls):
-    peers, count = X * CORES, Y * Z
-    rows, depth = normed.shape
-    tok = valid_row.shape[1]
-    lanes = len_row.shape[1]
-    native = w1.shape[1] // TILE
-    dma = pltpu.SemaphoreType.DMA
-    f32 = jnp.float32
-
-    def fixed(shape):
-        return pl.BlockSpec(shape, lambda j: (0, 0), pipeline_mode=pl.Buffered(1))
-
-    return pl.pallas_call(
-        functools.partial(scores_kernel, vocab, native),
-        grid=(native + w2.shape[1] // TILE,),
-        out_shape=(jax.ShapeDtypeStruct((1, rolls), f32), jax.ShapeDtypeStruct((1, tok), f32)),
-        in_specs=[
-            fixed((rows, depth)),
-            pl.BlockSpec((depth, TILE), lambda j: (0, jnp.minimum(j, native - 1))),
-            pl.BlockSpec((depth, TILE), lambda j: (0, jnp.maximum(j - native, 0))),
-            fixed((rows, 1)), fixed((1, tok)), fixed((1, lanes)), fixed((1, lanes)),
-        ],
-        out_specs=(pl.BlockSpec((1, rolls), lambda j: (0, 0)), pl.BlockSpec((1, tok), lambda j: (0, 0))),
-        scratch_shapes=[pltpu.VMEM((rows, 1), f32)] * 3
-        + [
-            pltpu.VMEM((8, rows), f32),
-            pltpu.VMEM((peers, 8, rows), f32),
-            pltpu.VMEM((8, lanes), f32),
-            pltpu.VMEM((count, 8, lanes), f32),
-            dma((peers,)), dma((peers,)), dma((count,)), dma((count,)),
-        ],
-        compiler_params=pltpu.CompilerParams(
-            collective_id=3, has_side_effects=True, vmem_limit_bytes=VMEM_BYTES
-        ),
-        cost_estimate=pl.CostEstimate(flops=8 * 10**9, bytes_accessed=2 * 10**7, transcendentals=10**6),
-        name="scores",
-    )(normed, w1, w2, target, valid_row, len_row, owner_row)
+        cost_estimate=pl.CostEstimate(flops=2 * 10**10, bytes_accessed=10**8, transcendentals=10**6),
+        name="finale",
+    )(
+        gated.reshape(models, X, CORES, share, inner), wo, wos, dw, dws, up, res, scale, head,
+        tgt, tgp, valid_row, len_row, owner_row,
+    )
 
 
 def shards(
@@ -731,9 +823,11 @@
     share = tok // (X * CORES)
     mp = lax.axis_index("mp")
     vocab = vocab_head_weight.shape[1]
-    head_native = lax.all_gather(vocab_head_weight[:, :HEAD_NATIVE], "seq", axis=0, tiled=True)
-    rest = vocab - HEAD_NATIVE
-    head_rest = jnp.pad(vocab_head_weight[:, HEAD_NATIVE:], ((0, 0), (0, -rest % TILE)))
+    half = -(-vocab // (2 * TILE)) * TILE
+    head = jnp.stack(
+        [vocab_head_weight[:, :half], jnp.pad(vocab_head_weight[:, half:], ((0, 0), (0, 2 * half - vocab)))]
+    )
+    target = jnp.broadcast_to(scored_token_targets.astype(jnp.float32)[None, :], (8, tok))
 
     def row(values, fill):
         return jnp.pad(values, (0, 128 - rolls), constant_values=fill)[None, :]
@@ -748,20 +842,16 @@
     y, run, ends, last = local_mix(
         len_row, x, b, c, jnp.transpose(token_step_sizes, (2, 0, 1)), head_decay_rate, head_skip_scale
     )
-    pall, en, dn, wos, dws = states(prompts, ends, last, shared_output_weight, adapter_down_weight)
+    pall, en, dn, wos, dws, target_p = states(
+        prompts, ends, last, shared_output_weight, adapter_down_weight, target
+    )
     gated = finish_mix(
         len_row, lengths[None, :], holders[None, :], y, run, c, z,
         pall.reshape((Z * Y,) + prompts.shape), en, dn,
     )
-    normed, head_own = project(
-        gated, shared_output_weight, wos, adapter_down_weight, dws, adapter_up_weight, own_res,
-        final_norm_scale[None, :], head_rest,
-    )
-    local = scored_token_targets - mp * vocab
-    target = jnp.concatenate([local, local])[:, None]
-    sums, delta = scores(
-        normed.reshape(models * tok, -1), head_native, head_own.reshape(-1, head_rest.shape[1]), vocab,
-        target, valid[None, :], len_row, owner_row, rolls,
+    sums, delta = finale(
+        vocab, gated, shared_output_weight, wos, adapter_down_weight, dws, adapter_up_weight, own_res,
+        final_norm_scale[None, :], head, target, target_p, valid[None, :], len_row, owner_row, rolls,
     )
     return sums, delta.reshape(tok)
 

time: 203 us -> 176 us (0.87)
  between operations: 14.1 us -> 0.69 us
  Pallas kernels: 176 us -> 164 us
  local copies, waits for them, and re-layouts: 11 us -> 8.03 us
    pallas_call x3 -> x2, Pallas kernels: 166 us -> 154 us  [the longest x1 107 us: finale(): pl.pallas_call(functools.partial(finale_kernel, vocab), out_shape=(jax.Sh...]
  transfers between devices with their start and end apart: 1 -> 0, of which waited for: 0 -> 0; matrix products, arithmetic and copies ran while one was open for 3% -> 0% of each run, Pallas kernels for 70% -> 0%
where the time goes in v3:
time: 176 us; the launch traced here: 173 us
  Pallas kernels  164 us (93%)
  local copies, waits for them, and re-layouts  8.03 us (5%)
    pallas_call x1, Pallas kernels, finale(): pl.pallas_call(functools.partial(finale_kernel, vocab), out_shape=(jax.Sh...  107 us
    pallas_call x1, Pallas kernels, states(): pl.pallas_call(states_kernel, out_shape=out, in_specs=[anywhere()] * 6, o...  46.6 us
    pallas_call x1, Pallas kernels, finish_mix(): pl.pallas_call(finish_mix_kernel, out_shape=jax.ShapeDtypeStruct((models,...  5.2 us
    pallas_call x1, Pallas kernels, local_mix(): pl.pallas_call(local_mix_kernel, out_shape=(jax.ShapeDtypeStruct((models,...  4.52 us

profile of v3, /device:TPU:0, one launch (start us, length us, event | category | flops | bytes accessed | tf_op | source)
XLA Modules:
  0.0 173.4 jit_solution(102113049096817983)
XLA Ops:
  0.6 1.2 pad_bitcast_fusion.1
  1.8 0.0 copy-start.3
  1.8 0.0 copy-start.1
  1.8 4.5 %local_mix.1 = (f32[2,448,256]{2,1,0:T(8,128)}, f32[2,8,256]{2,1,0:T(8,128)}, bf16[448,128]{1,0:T(8,128)(2,1)}, f32[8,128]{1,0:T(8,128)}) custom-call(s32[1,128]{1,0:T(1,128)} %get-tuple-element.29.len_ref, bf16[2,448,256]{2,1,0:T(8,128)(2,1)} %bitcast.35, bf16[2,64,256]{2,1,0:T(8,128)(2,1)} %bitcast.36, bf16[2,64,256]{2,1,0:T(8,128)(2,1)} %bitcast.30, ...), custom_call_target="tpu_custom_call" | custom-call | flops 2000000000 | bytes 4000000 | tf_op jit(solution)/shard_map/local_mix/pallas_call | solution.py:99
  6.3 0.0 copy-done.3
  6.4 0.6 broadcast_in_dim.27.tgt_ref
  6.9 0.0 copy-done.1
  6.9 0.2 copy.21
  7.2 0.8 reshape.17.pt_ref
  8.0 46.6 %state_exchange.1 = (bf16[8,4,448,128]{3,2,1,0:T(8,128)(2,1)}, bf16[4,448,128]{2,1,0:T(8,128)(2,1)}, f32[4,8,128]{2,1,0:T(8,128)}, bf16[448,3584]{1,0:T(8,128)(2...) custom-call(bf16[448,128]{1,0:T(8,128)(2,1)} %reshape.17.pt_ref, bf16[448,128]{1,0:T(8,128)(2,1)} %get-tuple-element.16.e_ref, ...), custom_call_target="tpu_custom_call" | custom-call | bytes 100000000 | tf_op jit(solution)/shard_map/state_exchange/pallas_call | solution.py:286
  54.6 0.0 copy-start
  54.6 0.0 slice-start
  54.6 0.0 copy-start.2
  54.7 5.2 %finish_mix.1 = bf16[2,256,448]{2,1,0:T(8,128)(2,1)} custom-call(s32[1,48]{1,0:T(1,128)} %bitcast.32, s32[1,48]{1,0:T(1,128)} %bitcast.34, s32[1,128]{1,0:T(1,128)} %get-tuple-element.29.len_ref, f32[2,448,256]{2,1,0:T(8,128)} %get-tuple-element.14.y_ref, f32[2,8,256]{2,1,0:T(8,128)} %get-tuple-element.15.run_ref, bf16[2,64,256]{2,1,0:T(8,128)(2,1)} %bitcast.31, ...), custom_call_target="tpu_custom_call" | custom-call | flops 1000000000 | bytes 8000000 | tf_op jit(solution)/shard_map/finish_mix/pallas_call | solution.py:381
  59.9 1.3 constant_dynamic-slice_fusion
  61.2 0.8 copy.25
  62.0 0.0 copy-done
  62.0 0.0 slice-done
  62.1 0.8 pad_maximum_fusion.head_ref
  62.9 0.0 copy-done.2
  62.9 0.6 broadcast_in_dim.28.scale_ref
  63.5 107.5 %finale.1 = (f32[1,48]{1,0:T(1,128)}, f32[1,256]{1,0:T(1,128)}) custom-call(bf16[2,4,2,32,448]{4,3,2,1,0:T(8,128)(2,1)} %bitcast.26, bf16[448,3584]{1,0:T(8,128)(2,1)} %wo_ref.3, bf16[448,3584]{1,0:T(8,128)(2,1)} %get-tuple-element.21.wos_ref, bf16[448,128]{1,0:T(8,128)(2,1)} %dw_ref.3, bf16[448,128]{1,0:T(8,128)(2,1)} %get-tuple-element.22.dws_ref, ...), custom_call_target="tpu_custom_call" | custom-call | flops 20000000000 | bytes 100000000 | tf_op jit(solution)/shard_map/finale/pallas_call | solution.py:779
  171.0 1.2 copy.28
  172.1 1.2 copy.29
  (2 shorter events, 0.0 us)
Async XLA Ops:
  1.8 4.5 %copy-start.3 = (s32[256]{0:T(256)S(1)}, s32[256]{0:T(256)}, u32[]{:S(2)}) copy-start(s32[256]{0:T(256)} %param.19) | copy-start | bytes 3076
  1.8 5.1 %copy-start.1 = (bf16[2,1,7,64,64]{4,3,2,1,0:T(8,128)(2,1)S(1)}, bf16[2,1,7,64,64]{4,3,2,1,0:T(8,128)(2,1)}, u32[]{:S(2)}) copy-start(bf16[2,1,7,64,64]{4,3,2,1,0:T(8,128)(2,1)} %param.31) | copy-start | bytes 344068
  54.6 7.4 %copy-start = (bf16[112,2000]{1,0:T(8,128)(2,1)S(1)}, bf16[112,2000]{1,0:T(8,128)(2,1)}, u32[]{:S(2)}) copy-start(bf16[112,2000]{1,0:T(8,128)(2,1)} %param.37) | copy-start | bytes 1344004
  54.6 7.4 %slice-start = ((bf16[112,2000]{1,0:T(8,128)(2,1)}), bf16[112,976]{1,0:T(8,128)(2,1)S(1)}, s32[]{:S(2)}) async-start(bf16[112,2000]{1,0:T(8,128)(2,1)} %param.37), calls=%async_computation | async-start | bytes 458752 | tf_op jit(solution)/shard_map/slice | solution.py:828
  54.6 8.2 %copy-start.2 = (f32[3584]{0:T(1024)S(1)}, f32[3584]{0:T(1024)}, u32[]{:S(2)}) copy-start(f32[3584]{0:T(1024)} %param.36) | copy-start | bytes 43012
